TPU v7x, 128 devices: a whole 4x4x4 slice. The times are simulated.
128 devices in a mesh: branch: 16 (over z, y_hi, core), scen: 8 (over x, y_lo).
Axes of the slice: x: 4, y: 4 (y_hi: 2, y_lo: 2; y = y_hi * 2 + y_lo), z: 4, core: 2. Of those that a mesh axis runs over, the one named last changes fastest.
Arguments:
- counts: int32 [128], P(('branch', 'scen')), may hold values from 1 to 4, as said below
- blocks: int32 [512], P(('branch', 'scen')), may hold values from 0 to 31, as said below
- factors: float32 [512, 512, 512], P(('branch', 'scen')), as said below
- b_first: float32 [512, 512, 512], P(('branch', 'scen')), may hold values from -0.2 to 0.2
- b_branch: float32 [512, 512, 512], P(('branch', 'scen')), may hold values from -0.8 to 0.8
- c_first: float32 [512, 512], replicated, may hold values from -6 to 6
- c_band: float32 [16384, 512], P(('branch', 'scen')), may hold values from -4 to 4
- c_diag: float32 [32, 512, 512], P('branch', 'scen'), may hold values from -6 to 6
Outputs:
- schur_first: float32 [512, 512], replicated
- schur_band: float32 [16384, 512], P(('branch', 'scen'))
- schur_diag: float32 [32, 512, 512], P('branch', 'scen')
Inputs may be any that keep to these rules, and one draw needn't show every extreme that they name: `counts`: every device holds one or more scenarios; some device holds 4. `blocks`: A slot of a device on branch index b names a block between 2 * b and 2 * b + 1. `factors`: each factor is lower triangular with a diagonal between 1 and 3 and off-diagonal entries of order 512 ** -0.5.
All inputs are finite; a program needn't handle non-finite values.
Results may differ from a plain program's by a relative error of at most 0.0003.
Values sent between devices are 32-bit elements; how exact they have to be, the bound alone decides.
A program may use at most 128 MiB of HBM per device.

v0:
```python
import jax
import jax.numpy as jnp
from jax import lax
from jax.sharding import PartitionSpec as P


def from_partner(value, axis, apart):
    mask = 2**apart
    pairs = [(source, source ^ mask) for source in range(lax.axis_size(axis))]
    return lax.ppermute(value, axis, pairs)


def scenario_terms(factor, first_cols, second_cols):
    block_width = first_cols.shape[1]
    rhs = jnp.concatenate([first_cols, second_cols], axis=1)
    solved = jax.scipy.linalg.solve_triangular(factor, rhs, lower=True)
    first_y = solved[:, :block_width]
    second_y = solved[:, block_width:]
    dims = (((0,), (0,)), ((), ()))
    first_term = lax.dot_general(
        first_y, first_y, dims, precision=lax.Precision.HIGHEST, preferred_element_type=jnp.float32
    )
    row_term = lax.dot_general(
        second_y, solved, dims, precision=lax.Precision.HIGHEST, preferred_element_type=jnp.float32
    )
    return (first_term, row_term)


def accumulate(lower_slot, upper_slot, slot_data, block_base, block_count, block_width):
    factor_set, first_set, second_set, block_set = slot_data

    def add_slot(slot_index, state_now):
        first_acc, row_acc = state_now
        first_term, row_term = scenario_terms(
            factor_set[slot_index], first_set[slot_index], second_set[slot_index]
        )
        local_block = block_set[slot_index] - block_base
        row_now = lax.dynamic_index_in_dim(row_acc, local_block, 0, keepdims=False)
        row_acc = lax.dynamic_update_index_in_dim(row_acc, row_now + row_term, local_block, 0)
        return (first_acc + first_term, row_acc)

    start_state = (
        jnp.zeros((block_width, block_width), jnp.float32),
        jnp.zeros((block_count, block_width, 2 * block_width), jnp.float32),
    )
    return lax.fori_loop(lower_slot, upper_slot, add_slot, start_state)


def shards(counts, blocks, factors, b_first, b_branch, c_first, c_band, c_diag):
    slot_count = factors.shape[0]
    block_width = b_first.shape[2]
    block_count = c_diag.shape[0]
    send_slots = (slot_count - 1) // 2
    branch_index = lax.axis_index("branch")
    own_count = counts[0]
    own_base = block_count * branch_index
    own_data = (factors, b_first, b_branch, blocks)
    branch_span = lax.axis_size("branch")
    top_bit = branch_span.bit_length() - 2
    send_start = jnp.maximum(own_count - send_slots, 0)
    outgoing = tuple(
        (lax.dynamic_slice_in_dim(array_in, send_start, send_slots, 0) for array_in in own_data)
    )
    incoming = from_partner(
        (counts, outgoing[0], outgoing[1], outgoing[2], outgoing[3]), "branch", top_bit
    )
    partner_count = incoming[0][0]
    give_count = jnp.maximum((own_count - partner_count) // 2, 0)
    take_count = jnp.maximum((partner_count - own_count) // 2, 0)
    own_first, own_rows = accumulate(
        0, own_count - give_count, own_data, own_base, block_count, block_width
    )
    in_factors, in_first, in_second = (incoming[1], incoming[2], incoming[3])

    def take_slot(slot_index, state_now):
        first_acc, term_set = state_now
        first_term, row_term = scenario_terms(
            in_factors[slot_index], in_first[slot_index], in_second[slot_index]
        )
        term_set = lax.dynamic_update_index_in_dim(term_set, row_term, slot_index, 0)
        return (first_acc + first_term, term_set)

    taken_start = (
        jnp.zeros((block_width, block_width), jnp.float32),
        jnp.zeros((send_slots, block_width, 2 * block_width), jnp.float32),
    )
    got_first, got_terms = lax.fori_loop(
        send_slots - take_count, send_slots, take_slot, taken_start
    )
    returned = from_partner(got_terms, "branch", top_bit)
    row_terms = own_rows
    local_block = outgoing[3][0] - own_base
    row_now = lax.dynamic_index_in_dim(row_terms, local_block, 0, keepdims=False)
    row_terms = lax.dynamic_update_index_in_dim(row_terms, row_now + returned[0], local_block, 0)
    first_local = own_first + got_first
    band_part = row_terms[:, :, :block_width].reshape(block_count * block_width, block_width)
    diag_part = row_terms[:, :, block_width:]
    band_sum, diag_sum = (
        lax.psum_scatter(band_part, "scen", scatter_dimension=0, tiled=True),
        lax.psum_scatter(diag_part, "scen", scatter_dimension=1, tiled=True),
    )
    first_total = lax.psum(first_local, ("branch", "scen"))
    return (c_first - first_total, c_band - band_sum, c_diag - diag_sum)


def solution(mesh):
    placed = (
        P(("branch", "scen")),
        P(("branch", "scen")),
        P(("branch", "scen"), None, None),
        P(("branch", "scen"), None, None),
        P(("branch", "scen"), None, None),
        P(),
        P(("branch", "scen"), None),
        P("branch", "scen", None),
    )
    return jax.shard_map(
        shards,
        mesh=mesh,
        in_specs=placed,
        out_specs=(P(), P(("branch", "scen"), None), P("branch", "scen", None)),
        check_vma=False,
    )
```

profile of v0, /device:TPU:1, one launch (start us, length us, event | category | flops | bytes accessed | tf_op | source)
XLA Modules:
  0.0 591.9 jit_solution(13948142097858505986)
XLA Ops:
  10.0 4.5 collective-permute-start.1
  14.6 2.3 constant_dynamic-slice_fusion.4
  16.9 2.9 collective-permute-start.2
  19.7 2.3 constant_dynamic-slice_fusion.3
  23.5 14.0 %collective-permute-done = s32[1]{0:T(128)} collective-permute-done((s32[1]{0:T(128)}, s32[1]{0:T(128)}, u32[]{:S(2)}, u32[]{:S(2)}) %collective-permute-start) | collective-permute-done | bytes 36 | tf_op jit(solution)/shard_map/ppermute | solution.py:10
  40.1 10.5 %while.34 = (s32[]{:T(128)}, f32[512,512]{1,0:T(8,128)S(1)}, s32[4,2]{0,1:T(2,128)S(1)}, f32[4,128,128]{2,1,0:T(8,128)}, s32[]{:T(128)}) while((s32[]{:T(128)}, f32[512,512]{1,0:T(8,128)S(1)}, s32[4,2]{0,1:T(2,128)S(1)}, f32[4,128,128]{2,1,0:T(8,128)}, s32[]{:T(128)}) %tuple.86), condition=%wide.while_cond.clone, body=%wide.while_body.clone.sunk | while | flops 2 | bytes 132205 | solution.py:16
  40.8 2.0 bitcast_dynamic-update-slice_fusion.7
  43.4 2.0 bitcast_dynamic-update-slice_fusion.7
  46.1 2.0 bitcast_dynamic-update-slice_fusion.7
  48.7 2.0 bitcast_dynamic-update-slice_fusion.7
  50.7 40.3 %custom-call.5 = f32[4,128,128]{1,2,0:T(8,128)S(1)} custom-call(f32[4,128,128]{2,1,0:T(8,128)} %get-tuple-element.143), custom_call_target="InvertDiagBlocksLowerTriangular" | custom-call | tf_op jit(solution)/shard_map/while/body/jit(_solve_triangular)/triangular_solve | solution.py:16
  96.2 2.9 fusion.36
  99.1 3.6 fusion.34
  104.5 2.7 collective-permute-start.4
  108.3 2.5 broadcast_in_dim.18
  110.7 215.1 %while.32 = (s32[]{:T(128)}, f32[512,512]{1,0:T(8,128)}, f32[2,512,1024]{2,1,0:T(8,128)}, s32[]{:T(128)}, f32[4,512,512]{2,1,0:T(8,128)}, /*index=5*/f32[4,512,5...) while((s32[]{:T(128)}, f32[512,512]{1,0:T(8,128)}, ...), condition=%wide.region_1.3_spmd, body=%wide.region_0.2_spmd.sunk | while | flops 6849953792 | bytes 84674112 | solution.py:46
  113.8 10.5 %while.35 = (s32[]{:T(128)}, f32[512,512]{1,0:T(8,128)S(1)}, s32[4,2]{0,1:T(2,128)S(1)}, f32[4,128,128]{2,1,0:T(8,128)}, s32[]{:T(128)}) while((s32[]{:T(128)}, f32[512,512]{1,0:T(8,128)S(1)}, s32[4,2]{0,1:T(2,128)S(1)}, f32[4,128,128]{2,1,0:T(8,128)}, s32[]{:T(128)}) %tuple.80), condition=%wide.while_cond, body=%wide.while_body.sunk | while | flops 2 | bytes 132205 | solution.py:16
  114.5 2.0 bitcast_dynamic-update-slice_fusion.8
  117.1 2.0 bitcast_dynamic-update-slice_fusion.8
  119.7 2.0 bitcast_dynamic-update-slice_fusion.8
  122.3 2.0 bitcast_dynamic-update-slice_fusion.8
  124.3 40.1 %custom-call.11 = f32[4,128,128]{1,2,0:T(8,128)S(1)} custom-call(f32[4,128,128]{2,1,0:T(8,128)} %get-tuple-element.336), custom_call_target="InvertDiagBlocksLowerTriangular" | custom-call | tf_op jit(solution)/shard_map/while/body/jit(_solve_triangular)/triangular_solve | solution.py:16
  170.7 2.1 convolution_add_fusion.2
  176.9 3.6 bitcast_dynamic-update-slice_fusion.6
  180.5 1.9 copy-done.1
  185.5 10.5 %while.35 = (s32[]{:T(128)}, f32[512,512]{1,0:T(8,128)S(1)}, s32[4,2]{0,1:T(2,128)S(1)}, f32[4,128,128]{2,1,0:T(8,128)}, s32[]{:T(128)}) while((s32[]{:T(128)}, f32[512,512]{1,0:T(8,128)S(1)}, s32[4,2]{0,1:T(2,128)S(1)}, f32[4,128,128]{2,1,0:T(8,128)}, s32[]{:T(128)}) %tuple.80), condition=%wide.while_cond, body=%wide.while_body.sunk | while | flops 2 | bytes 132205 | solution.py:16
  186.2 2.0 bitcast_dynamic-update-slice_fusion.8
  188.8 2.0 bitcast_dynamic-update-slice_fusion.8
  191.4 2.0 bitcast_dynamic-update-slice_fusion.8
  194.0 2.0 bitcast_dynamic-update-slice_fusion.8
  196.0 40.1 %custom-call.11 = f32[4,128,128]{1,2,0:T(8,128)S(1)} custom-call(f32[4,128,128]{2,1,0:T(8,128)} %get-tuple-element.336), custom_call_target="InvertDiagBlocksLowerTriangular" | custom-call | tf_op jit(solution)/shard_map/while/body/jit(_solve_triangular)/triangular_solve | solution.py:16
  242.3 2.1 convolution_add_fusion.2
  248.6 3.6 bitcast_dynamic-update-slice_fusion.6
  252.2 1.9 copy-done.1
  257.2 10.5 %while.35 = (s32[]{:T(128)}, f32[512,512]{1,0:T(8,128)S(1)}, s32[4,2]{0,1:T(2,128)S(1)}, f32[4,128,128]{2,1,0:T(8,128)}, s32[]{:T(128)}) while((s32[]{:T(128)}, f32[512,512]{1,0:T(8,128)S(1)}, s32[4,2]{0,1:T(2,128)S(1)}, f32[4,128,128]{2,1,0:T(8,128)}, s32[]{:T(128)}) %tuple.80), condition=%wide.while_cond, body=%wide.while_body.sunk | while | flops 2 | bytes 132205 | solution.py:16
  257.9 2.0 bitcast_dynamic-update-slice_fusion.8
  260.5 2.0 bitcast_dynamic-update-slice_fusion.8
  263.1 2.0 bitcast_dynamic-update-slice_fusion.8
  265.7 2.0 bitcast_dynamic-update-slice_fusion.8
  267.7 40.1 %custom-call.11 = f32[4,128,128]{1,2,0:T(8,128)S(1)} custom-call(f32[4,128,128]{2,1,0:T(8,128)} %get-tuple-element.336), custom_call_target="InvertDiagBlocksLowerTriangular" | custom-call | tf_op jit(solution)/shard_map/while/body/jit(_solve_triangular)/triangular_solve | solution.py:16
  314.0 2.1 convolution_add_fusion.2
  320.3 3.6 bitcast_dynamic-update-slice_fusion.6
  323.9 1.9 copy-done.1
  325.8 2.7 add.64
  328.6 4.1 add_dynamic-update-slice_fusion
  332.7 4.7 fusion.69
  338.0 240.6 %all-reduce.2.cloned.1.call-done = f32[512,512]{1,0:T(8,128)} async-done(((f32[512,512]{1,0:T(8,128)}), f32[512,512]{1,0:T(8,128)}) %all-reduce.2.cloned.1.call-update) | async-done | bytes 1048592 | tf_op jit(solution)/shard_map/psum | solution.py:102
  578.6 2.4 sub.44
  (142 shorter events, 63.8 us)
Async XLA Ops:
  8.0 570.6 %all-reduce.2.cloned.1.call-start = ((), (), s32[]{:S(2)}) async-start(), calls=%async_computation.2 | async-start | bytes 2097152 | tf_op jit(solution)/shard_map/psum | solution.py:102
  10.0 12.1 %copy-start.8 = (s32[4]{0:T(128)S(1)}, s32[4]{0:T(128)}, u32[]{:S(2)}) copy-start(s32[4]{0:T(128)} %param.15) | copy-start | bytes 52
  10.0 28.8 %collective-permute-start.1 = (f32[1,512,512]{2,1,0:T(8,128)S(1)}, f32[1,512,512]{2,1,0:T(8,128)}, u32[]{:S(2)}, u32[]{:S(2)}) collective-permute-start(f32[1,512,512]{2,1,0:T(8,128)S(1)} %constant_dynamic-slice_fusion.5), channel_id=1, source_target_pairs={{0,64},{8,72},{16,80},{24,88},{32,96},{40,104},{48,112},{56,120},{... | collective-permute-start | bytes 3145736 | tf_op jit(solution)/shard_map/ppermute | solution.py:10
  14.5 23.0 %collective-permute-start = (s32[1]{0:T(128)}, s32[1]{0:T(128)}, u32[]{:S(2)}, u32[]{:S(2)}) collective-permute-start(s32[1]{0:T(128)} %param.14), channel_id=1, source_target_pairs={{0,64},{8,72},{16,80},{24,88},{32,96},{40,104},{48,112},{56,120},{... | collective-permute-start | bytes 20 | tf_op jit(solution)/shard_map/ppermute | solution.py:10
  16.9 74.1 %collective-permute-start.2 = (f32[1,512,512]{2,1,0:T(8,128)}, f32[1,512,512]{2,1,0:T(8,128)S(1)}, u32[]{:S(2)}, u32[]{:S(2)}) collective-permute-start(f32[1,512,512]{2,1,0:T(8,128)} %constant_dynamic-slice_fusion.4), channel_id=1, source_target_pairs={{0,64},{8,72},{16,80},{24,88},{32,96},{40,104},{48,112},{56,120},{... | collective-permute-start | bytes 3145736 | tf_op jit(solution)/shard_map/ppermute | solution.py:10
  22.0 69.0 %collective-permute-start.3 = (f32[1,512,512]{2,1,0:T(8,128)}, f32[1,512,512]{2,1,0:T(8,128)S(1)}, u32[]{:S(2)}, u32[]{:S(2)}) collective-permute-start(f32[1,512,512]{2,1,0:T(8,128)} %constant_dynamic-slice_fusion.3), channel_id=1, source_target_pairs={{0,64},{8,72},{16,80},{24,88},{32,96},{40,104},{48,112},{56,120},{... | collective-permute-start | bytes 3145736 | tf_op jit(solution)/shard_map/ppermute | solution.py:10
  104.5 6.3 %copy-start.2 = (f32[512,512]{1,0:T(8,128)}, f32[512,512]{1,0:T(8,128)S(1)}, u32[]{:S(2)}) copy-start(f32[512,512]{1,0:T(8,128)S(1)} %get-tuple-element.125) | copy-start | bytes 3145732
  104.5 224.1 %collective-permute-start.4 = (f32[1,512,1024]{2,1,0:T(8,128)}, f32[1,512,1024]{2,1,0:T(8,128)}, u32[]{:S(2)}, u32[]{:S(2)}) collective-permute-start(f32[1,512,1024]{2,1,0:T(8,128)} %get-tuple-element.127), channel_id=1, source_target_pairs={{0,64},{8,72},{16,80},{24,88},{32,96},{40,104},{48,112},{56,120},{... | collective-permute-start | bytes 6291464 | tf_op jit(solution)/shard_map/ppermute | solution.py:10
  169.4 1.2 copy-start.3
  172.8 3.2 copy-start.4
  174.1 2.8 copy-start
  180.5 1.9 copy-start.1
  241.1 1.2 copy-start.3
  244.5 3.2 copy-start.4
  245.8 2.8 copy-start
  252.2 1.9 copy-start.1
  312.8 1.2 copy-start.3
  316.2 3.2 copy-start.4
  317.5 2.8 copy-start
  323.9 1.9 copy-start.1
  328.6 252.5 %reduce-scatter.3.cloned.1.call-start = ((), (), s32[]{:S(2)}) async-start(), calls=%async_computation.3 | async-start | bytes 2359296 | tf_op jit(solution)/shard_map/reduce_scatter | solution.py:99
  337.4 241.2 %copy-start.5 = (f32[512,512]{1,0:T(8,128)S(1)}, f32[512,512]{1,0:T(8,128)}, u32[]{:S(2)}) copy-start(f32[512,512]{1,0:T(8,128)} %param.19) | copy-start | bytes 3145732
  337.4 245.3 %reduce-scatter.5.cloned.1.call-start = ((), (), s32[]{:S(2)}) async-start(), calls=%async_computation.4 | async-start | bytes 2359296 | tf_op jit(solution)/shard_map/reduce_scatter | solution.py:100
  338.0 243.0 %copy-start.6 = (f32[128,512]{1,0:T(8,128)S(1)}, f32[128,512]{1,0:T(8,128)}, u32[]{:S(2)}) copy-start(f32[128,512]{1,0:T(8,128)} %param.20) | copy-start | bytes 786436
  338.0 244.7 %copy-start.7 = (f32[2,64,512]{2,1,0:T(8,128)S(1)}, f32[2,64,512]{2,1,0:T(8,128)}, u32[]{:S(2)}) copy-start(f32[2,64,512]{2,1,0:T(8,128)} %param.21) | copy-start | bytes 786436
Sparse Core Ops, SparseCore 0:
  328.7 249.8 all-reduce.1
Sparse Core Ops, SparseCore 1:
  337.5 123.2 reduce-scatter.2
  463.0 53.2 reduce-scatter.4
where the time goes:
time: 592 us
  waiting for transfers between devices  255 us (43%)
  other arithmetic  179 us (30%)
  local copies, waits for them, and re-layouts  82.9 us (14%)
  matrix products  43.3 us (7%)
  between operations  18.3 us (3%)
  starting transfers between devices  10.4 us (2%)
    psum x1, waiting for transfers between devices, shards(): first_total = lax.psum(first_local, ('branch', 'scen'))  241 us
    another operation x20, other arithmetic, scenario_terms(): solved = jax.scipy.linalg.solve_triangular(factor, rhs, lower=True)  167 us
    another operation x52, local copies, waits for them, and re-layouts, scenario_terms(): solved = jax.scipy.linalg.solve_triangular(factor, rhs, lower=True)  41.8 us
    another operation x28, matrix products, scenario_terms(): solved = jax.scipy.linalg.solve_triangular(factor, rhs, lower=True)  19.8 us
    dot_general x4, matrix products, scenario_terms(): lax.dot_general(second_y, solved, dims, precision=lax.Precision.HIGHEST,...  14.3 us
    ppermute x5, waiting for transfers between devices, from_partner(): return lax.ppermute(value, axis, pairs)  14 us
  transfers between devices with their start and end apart: 8, of which 2 were waited for; matrix products, arithmetic and copies ran while one was open for 47% of the time, Pallas kernels for 0%

commit v1 on v0

v1 whole, which is shorter than its diff:
```python
import jax
import jax.numpy as jnp
from jax import lax
from jax.experimental import pallas as pl
from jax.experimental.pallas import tpu as pltpu
from jax.sharding import PartitionSpec as P

F32, BF16 = jnp.float32, jnp.bfloat16


def split(value):
    high = value.astype(BF16)
    return high, (value - high.astype(F32)).astype(BF16)


def dot3(left, right, dims):
    (lh, ll), (rh, rl) = left, right
    one = lambda a, b: lax.dot_general(a, b, (dims, ((), ())), preferred_element_type=F32)
    return one(lh, rl) + one(ll, rh) + one(lh, rh)


NN = ((1,), (0,))
TN = ((0,), (0,))


def on_diagonal(wide):
    lane = lax.broadcasted_iota(jnp.int32, wide.shape, 1)
    left = lane < wide.shape[0]
    zero = jnp.zeros_like(wide)
    return jnp.concatenate([jnp.where(left, wide, zero), jnp.where(left, zero, wide)], axis=0)


def pair_inverses(wides):
    rows, cols = wides[0].shape
    r = lax.broadcasted_iota(jnp.int32, (rows, cols), 0)
    c = lax.broadcasted_iota(jnp.int32, (rows, cols), 1) & (rows - 1)
    eye = r == c
    out = []
    for wide in wides:
        pivots = jnp.where(eye, wide, 0.0)
        by_col = 1.0 / jnp.sum(pivots, axis=0, keepdims=True)
        by_row = 1.0 / jnp.concatenate(
            [
                jnp.broadcast_to(jnp.sum(pivots[:, i : i + rows], axis=1, keepdims=True), (rows, rows))
                for i in range(0, cols, rows)
            ],
            axis=1,
        )
        pairs = ((r >> 1) == (c >> 1)) & (r > c)
        out.append(jnp.where(eye, by_row, 0.0) - jnp.where(pairs, wide * by_col * by_row, 0.0))
    shift = 1
    while (1 << shift) < rows:
        below = ((r >> (shift + 1)) == (c >> (shift + 1))) & ((r >> shift) > (c >> shift))
        inv = [split(x) for x in out]
        inv_on = [split(on_diagonal(x)) for x in out]
        mid = [dot3(split(jnp.where(below, w, 0.0)), x, NN) for w, x in zip(wides, inv_on)]
        mid_on = [split(on_diagonal(m)) for m in mid]
        out = [x - dot3(xs, m, NN) for x, xs, m in zip(out, inv, mid_on)]
        shift += 1
    return out


def half_inverses(factor, half):
    q = half // 2
    wides = []
    for start in (0, half):
        a = factor[start : start + q, start : start + q]
        d = factor[start + q : start + half, start + q : start + half]
        wides.append(jnp.concatenate([a, d], axis=1))
    invs = pair_inverses(wides)
    full = []
    for start, wide in zip((0, half), invs):
        a, d = split(wide[:, :q]), split(wide[:, q:])
        low = split(factor[start + q : start + half, start : start + q])
        corner = -dot3(d, split(dot3(low, a, NN)), NN)
        top = jnp.concatenate([wide[:, :q], jnp.zeros((q, q), F32)], axis=1)
        full.append(jnp.concatenate([top, jnp.concatenate([corner, wide[:, q:]], axis=1)], axis=0))
    return full


def compute_kernel(counts, blocks, fac_hbm, bf_hbm, bb_hbm, first, band, diag, fac, rhs, yh, yl, sems):
    n, w = fac_hbm.shape[1], bf_hbm.shape[2]
    half = n // 2
    live = counts[0]

    def loads(s):
        return (
            pltpu.make_async_copy(fac_hbm.at[s], fac.at[s], sems.at[s, 0]),
            pltpu.make_async_copy(bf_hbm.at[s], rhs.at[s, :, pl.ds(0, w)], sems.at[s, 1]),
            pltpu.make_async_copy(bb_hbm.at[s], rhs.at[s, :, pl.ds(w, w)], sems.at[s, 2]),
        )

    @pl.loop(0, live)
    def _(s):
        for copy in loads(s):
            copy.start()

    first[...] = jnp.zeros_like(first)
    band[...] = jnp.zeros_like(band)
    diag[...] = jnp.zeros_like(diag)

    @pl.loop(0, live)
    def _(s):
        load_f, load_a, load_b = loads(s)
        load_f.wait()
        factor = fac.at[s]
        inv_top, inv_low = (split(x) for x in half_inverses(factor, half))
        link = split(factor[half:, :half])
        load_a.wait()
        load_b.wait()
        for col in range(0, 2 * w, half):
            cols = pl.ds(col, half)
            top = dot3(inv_top, split(rhs[s, :half, cols]), NN)
            top_s = split(top)
            yh[:half, cols], yl[:half, cols] = top_s
            low = dot3(inv_low, split(rhs[s, half:, cols] - dot3(link, top_s, NN)), NN)
            yh[half:, cols], yl[half:, cols] = split(low)
        k = blocks[s] & 1
        for i in range(0, 2 * w, half):
            left = (yh[:, pl.ds(i, half)], yl[:, pl.ds(i, half)])
            for j in range(0, i + half, half):
                if i >= w and j >= w and j > i:
                    continue
                right = (yh[:, pl.ds(j, half)], yl[:, pl.ds(j, half)])
                term = dot3(left, right, TN)
                if i < w:
                    first[pl.ds(i, half), pl.ds(j, half)] += term
                elif j < w:
                    band[k, pl.ds(i - w, half), pl.ds(j, half)] += term
                else:
                    diag[k, pl.ds(i - w, half), pl.ds(j - w, half)] += term

    first[:half, half:] = first[half:, :half].T
    for k in range(diag.shape[0]):
        diag[k, :half, half:] = diag[k, half:, :half].T


def local_sums(counts, blocks, factors, b_first, b_branch, block_count):
    cap, n, w = b_first.shape
    smem = pl.BlockSpec(memory_space=pltpu.SMEM)
    hbm = pl.BlockSpec(memory_space=pl.ANY)
    vmem = pl.BlockSpec(memory_space=pltpu.VMEM)
    return pl.pallas_call(
        compute_kernel,
        out_shape=(
            jax.ShapeDtypeStruct((w, w), F32),
            jax.ShapeDtypeStruct((block_count, w, w), F32),
            jax.ShapeDtypeStruct((block_count, w, w), F32),
        ),
        in_specs=[smem, smem, hbm, hbm, hbm],
        out_specs=(vmem, vmem, vmem),
        scratch_shapes=[
            pltpu.VMEM((cap, n, n), F32),
            pltpu.VMEM((cap, n, 2 * w), F32),
            pltpu.VMEM((n, 2 * w), BF16),
            pltpu.VMEM((n, 2 * w), BF16),
            pltpu.SemaphoreType.DMA((cap, 3)),
        ],
        compiler_params=pltpu.CompilerParams(vmem_limit_bytes=48 << 20),
        name="local_sums",
    )(counts, blocks, factors, b_first, b_branch)


def shards(counts, blocks, factors, b_first, b_branch, c_first, c_band, c_diag):
    first, band, diag = local_sums(counts, blocks, factors, b_first, b_branch, c_diag.shape[0])
    band = band.reshape(-1, band.shape[-1])
    band_sum = lax.psum_scatter(band, "scen", scatter_dimension=0, tiled=True)
    diag_sum = lax.psum_scatter(diag, "scen", scatter_dimension=1, tiled=True)
    first_sum = lax.psum(first, ("branch", "scen"))
    return (c_first - first_sum, c_band - band_sum, c_diag - diag_sum)


def solution(mesh):
    placed = (
        P(("branch", "scen")),
        P(("branch", "scen")),
        P(("branch", "scen"), None, None),
        P(("branch", "scen"), None, None),
        P(("branch", "scen"), None, None),
        P(),
        P(("branch", "scen"), None),
        P("branch", "scen", None),
    )
    return jax.shard_map(
        shards,
        mesh=mesh,
        in_specs=placed,
        out_specs=(P(), P(("branch", "scen"), None), P("branch", "scen", None)),
        check_vma=False,
    )
```

time: 592 us -> 247 us (0.42)
  other arithmetic: 179 us -> 5.78 us
  local copies, waits for them, and re-layouts: 82.9 us -> 0.67 us
  waiting for transfers between devices: 255 us -> 195 us
  matrix products: 43.3 us -> 0 us
  Pallas kernels: 0 us -> 28.7 us
  starting transfers between devices: 10.4 us -> 0.12 us
    another operation x20 -> x0, other arithmetic: 167 us -> none  [scenario_terms(): solved = jax.scipy.linalg.solve_triangular(factor, rhs, lower=True)]
    psum x1, waiting for transfers between devices: 241 us -> 194 us  [shards(): first_sum = lax.psum(first, ('branch', 'scen'))]
    another operation x54 -> x0, local copies, waits for them, and re-layouts: 43 us -> none  [the longest x52 41.8 us: scenario_terms(): solved = jax.scipy.linalg.solve_triangular(factor, rhs, lower=True)]
    pallas_call x0 -> x1, Pallas kernels: none -> 28.7 us  [local_sums(): pl.pallas_call(compute_kernel, out_shape=(jax.ShapeDtypeStruct((w, w), F3...]
    dot_general x8 -> x0, matrix products: 23.5 us -> none  [the longest x4 14.3 us: scenario_terms(): lax.dot_general(second_y, solved, dims, precision=lax.Precision.HIGHEST,...]
    another operation x28 -> x0, matrix products: 19.8 us -> none  [scenario_terms(): solved = jax.scipy.linalg.solve_triangular(factor, rhs, lower=True)]
    dynamic_slice x10 -> x0, local copies, waits for them, and re-layouts: 14.2 us -> none  [the longest x4 6.52 us: shards(): lax.dynamic_slice_in_dim(array_in, send_start, send_slots, 0)]
    ppermute x5 -> x0, waiting for transfers between devices: 14 us -> none  [from_partner(): return lax.ppermute(value, axis, pairs)]
  transfers between devices with their start and end apart: 8 -> 3, of which waited for: 2 -> 1; matrix products, arithmetic and copies ran while one was open for 47% -> 2% of each run, Pallas kernels for 0% -> 0%
where the time goes in v1:
time: 247 us; the launch traced here: 246 us
  waiting for transfers between devices  195 us (79%)
  Pallas kernels  28.7 us (12%)
  between operations  16.2 us (7%)
  other arithmetic  5.78 us (2%)
    psum x1, waiting for transfers between devices, shards(): first_sum = lax.psum(first, ('branch', 'scen'))  194 us
    pallas_call x1, Pallas kernels, local_sums(): pl.pallas_call(compute_kernel, out_shape=(jax.ShapeDtypeStruct((w, w), F3...  28.7 us
    sub x3, other arithmetic, shards(): return (c_first - first_sum, c_band - band_sum, c_diag - diag_sum)  5.78 us
  transfers between devices with their start and end apart: 3, of which 1 were waited for; matrix products, arithmetic and copies ran while one was open for 2% of the time, Pallas kernels for 0%

profile of v1, /device:TPU:1, one launch (start us, length us, event | category | flops | bytes accessed | tf_op | source)
XLA Modules:
  0.0 246.5 jit_solution(2844322438333092649)
XLA Ops:
  8.0 0.0 all-reduce.2.cloned.1.call-start
  8.7 0.0 copy-start
  8.7 0.6 copy-done
  9.3 28.7 %local_sums.1 = (f32[512,512]{1,0:T(8,128)}, f32[2,512,512]{2,1,0:T(8,128)}, f32[2,512,512]{2,1,0:T(8,128)}) custom-call(s32[1]{0:T(128)S(6)} %copy.12.counts, s32[4]{0:T(128)S(1)} %copy-done, f32[4,512,512]{2,1,0:T(8,128)} %fac_hbm.1, f32[4,512,512]{2,1,0:T(8,128)} %bf_hbm.1, f32[4,512,512]{2,1,0:T(8,128)} %bb_hbm.1), custom_call_target="tpu_custom_call" | custom-call | tf_op jit(solution)/shard_map/local_sums/pallas_call | solution.py:143
  38.1 0.0 copy-start.1
  38.1 0.0 copy-start.2
  38.1 0.0 all-reduce.2.cloned.1.call-update
  38.1 0.0 copy-start.3
  38.1 0.0 reduce-scatter.3.cloned.1.call-start
  38.2 0.5 reduce-scatter.3.cloned.1.call-update
  38.7 0.0 reduce-scatter.5.cloned.1.call-start
  38.8 0.5 reduce-scatter.5.cloned.1.call-update
  39.3 193.9 %all-reduce.2.cloned.1.call-done = f32[512,512]{1,0:T(8,128)} async-done(((f32[512,512]{1,0:T(8,128)}), f32[512,512]{1,0:T(8,128)}) %all-reduce.2.cloned.1.call-update) | async-done | bytes 1048592 | tf_op jit(solution)/shard_map/psum | solution.py:169
  233.2 0.0 copy-done.1
  233.2 2.4 sub.9
  235.6 0.0 reduce-scatter.3.cloned.1.call-done
  235.6 0.0 copy-done.2
  235.6 1.7 sub.10
  237.3 0.0 reduce-scatter.5.cloned.1.call-done
  237.3 0.0 copy-done.3
  237.3 1.7 sub.11
Async XLA Ops:
  8.0 225.2 %all-reduce.2.cloned.1.call-start = ((), (), s32[]{:S(2)}) async-start(), calls=%async_computation.2 | async-start | bytes 2097152 | tf_op jit(solution)/shard_map/psum | solution.py:169
  8.7 0.7 copy-start
  38.1 195.2 %copy-start.1 = (f32[512,512]{1,0:T(8,128)S(1)}, f32[512,512]{1,0:T(8,128)}, u32[]{:S(2)}) copy-start(f32[512,512]{1,0:T(8,128)} %param.13) | copy-start | bytes 3145732
  38.1 197.6 %copy-start.2 = (f32[128,512]{1,0:T(8,128)S(1)}, f32[128,512]{1,0:T(8,128)}, u32[]{:S(2)}) copy-start(f32[128,512]{1,0:T(8,128)} %param.14) | copy-start | bytes 786436
  38.1 199.2 %copy-start.3 = (f32[2,64,512]{2,1,0:T(8,128)S(1)}, f32[2,64,512]{2,1,0:T(8,128)}, u32[]{:S(2)}) copy-start(f32[2,64,512]{2,1,0:T(8,128)} %param.15) | copy-start | bytes 786436
  38.1 197.5 %reduce-scatter.3.cloned.1.call-start = ((), (), s32[]{:S(2)}) async-start(), calls=%async_computation.3 | async-start | bytes 2359296 | tf_op jit(solution)/shard_map/reduce_scatter | solution.py:167
  38.7 198.6 %reduce-scatter.5.cloned.1.call-start = ((), (), s32[]{:S(2)}) async-start(), calls=%async_computation.4 | async-start | bytes 2359296 | tf_op jit(solution)/shard_map/reduce_scatter | solution.py:168
Sparse Core Ops, SparseCore 0:
  38.2 194.9 all-reduce.1
Sparse Core Ops, SparseCore 1:
  41.0 61.1 reduce-scatter.2
  104.5 53.2 reduce-scatter.4

commit v2 on v1

--- a/solution.py
+++ b/solution.py
@@ -161,13 +161,256 @@
     )(counts, blocks, factors, b_first, b_branch)
 
 
+class Net:
+    def __init__(self, send_sems, recv_sems):
+        self.sems = (send_sems, recv_sems)
+        self.count = 0
+        self.sent = []
+
+    def send(self, source, target, device):
+        copy = pltpu.make_async_remote_copy(
+            src_ref=source,
+            dst_ref=target,
+            send_sem=self.sems[0].at[self.count],
+            recv_sem=self.sems[1].at[self.count],
+            device_id=device,
+            device_id_type=pl.DeviceIdType.MESH,
+        )
+        copy.start()
+        self.count += 1
+        self.sent.append(copy)
+        return copy
+
+    def drain(self):
+        for copy in self.sent:
+            copy.wait_send()
+
+
+FAR, NEXT, PREV, OWN = 0, 1, 2, 3
+OFFSETS = (2, 1, 3, 0)
+
+
+class Ring:
+    def __init__(self, net, piece, up, down, far_in, out, near_in):
+        self.net, self.piece, self.up, self.down = net, piece, up, down
+        self.far_in, self.out, self.near_in = far_in, out, near_in
+
+    def far(self):
+        self.far_up = self.net.send(self.piece(FAR, 0), self.far_in.at[0], self.up)
+        self.far_down = self.net.send(self.piece(FAR, 1), self.far_in.at[1], self.down)
+
+    def near_up(self):
+        self.n01 = self.net.send(self.piece(NEXT, 1), self.near_in.at[0, 1], self.up)
+
+    def near_down(self):
+        self.n10 = self.net.send(self.piece(PREV, 0), self.near_in.at[1, 0], self.down)
+
+    def mid_up(self):
+        self.far_up.wait_recv()
+        self.out[0] = self.piece(NEXT, 0)[...] + self.far_in[0]
+        self.n00 = self.net.send(self.out.at[0], self.near_in.at[0, 0], self.up)
+
+    def mid_down(self):
+        self.far_down.wait_recv()
+        self.out[1] = self.piece(PREV, 1)[...] + self.far_in[1]
+        self.n11 = self.net.send(self.out.at[1], self.near_in.at[1, 1], self.down)
+
+    def end(self):
+        for copy in (self.n01, self.n10, self.n00, self.n11):
+            copy.wait_recv()
+        return [self.piece(OWN, h)[...] + self.near_in[0, h] + self.near_in[1, h] for h in range(2)]
+
+
+def exchange_kernel(
+    first, band, diag, cf_hbm, cb_hbm, cd_hbm, out_f, out_b, out_d,
+    cf, cb, cd, core_in, held, z_far, z_out, z_near, z_sum, y_in, x_all, full,
+    b_far, b_out, b_near, b_send, b_in, b_keep, d_in, d_far, d_out, d_near, send_sems, recv_sems, c_sems,
+):
+    b, s = lax.axis_index("branch"), lax.axis_index("scen")
+    z, y_hi, core = b // 4, (b // 2) % 2, b % 2
+    x, y_lo = s // 2, s % 2
+    y = 2 * y_hi + y_lo
+    w = first.shape[1]
+    half = w // 2
+    halves = (pl.ds(0, half), pl.ds(half, half))
+    net = Net(send_sems, recv_sems)
+
+    other_core = (b + 1 - 2 * core, s)
+    z_up, z_down = (((z + 1) % 4) * 4 + b % 4, s), (((z + 3) % 4) * 4 + b % 4, s)
+    y_peers = []
+    for d in (1, 2, 3):
+        there = (y + d) % 4
+        y_peers.append((z * 4 + (there // 2) * 2 + core, x * 2 + there % 2))
+    x_peers = [(b, ((x + d) % 4) * 2 + y_lo) for d in (1, 2, 3)]
+    x_up, x_down = x_peers[0], x_peers[2]
+    y_near = (b, x * 2 + 1 - y_lo)
+
+    c_copies = [
+        pltpu.make_async_copy(source, target, c_sems.at[i])
+        for i, (source, target) in enumerate(((cf_hbm, cf), (cb_hbm, cb), (cd_hbm, cd)))
+    ]
+    for copy in c_copies:
+        copy.start()
+
+    barrier = pltpu.get_barrier_semaphore()
+    greeted = [other_core, z_up, z_down] + y_peers + x_peers
+    for peer in greeted:
+        pl.semaphore_signal(barrier, inc=1, device_id=peer, device_id_type=pl.DeviceIdType.MESH)
+    pl.semaphore_wait(barrier, len(greeted))
+
+    rows_core = pl.multiple_of(core * half, half)
+    core_rows, core_far = pl.ds(rows_core, half), pl.ds(pl.multiple_of((1 - core) * half, half), half)
+    core_copy = net.send(first.at[core_far], core_in, other_core)
+
+    sub = band.shape[0] // 8
+    bands = []
+    for chunk, y_to in enumerate((1 - y_lo, y_lo)):
+
+        def band_piece(role, h, y_to=y_to):
+            start = ((x + OFFSETS[role]) % 4) * (2 * sub) + y_to * sub
+            return band.at[pl.ds(pl.multiple_of(start, sub), sub), halves[h]]
+
+        bands.append(Ring(net, band_piece, x_up, x_down, b_far.at[chunk], b_out.at[chunk], b_near.at[chunk]))
+    drow = diag.shape[1] // 8
+
+    def diag_rows(role, y_to):
+        start = ((x + OFFSETS[role]) % 4) * (2 * drow) + y_to * drow
+        return diag.at[:, pl.ds(pl.multiple_of(start, drow), drow), :]
+
+    def diag_send(role):
+        return net.send(diag_rows(role, 1 - y_lo), d_in.at[role], y_near)
+
+    def diag_take(copy, role):
+        copy.wait_recv()
+        d_in[role] += diag_rows(role, y_lo)[...]
+
+    diags = Ring(net, lambda role, h: d_in.at[role, :, :, halves[h]], x_up, x_down, d_far, d_out, d_near)
+
+    zrow = half // 4
+    z_ring = Ring(
+        net,
+        lambda role, h: held.at[pl.ds(pl.multiple_of(((z + OFFSETS[role]) % 4) * zrow, zrow), zrow), halves[h]],
+        z_up, z_down, z_far, z_out, z_near,
+    )
+
+    bands[0].far()
+    d0 = diag_send(FAR)
+    bands[1].far()
+    bands[0].near_up()
+    bands[0].near_down()
+
+    core_copy.wait_recv()
+    held[...] = first[core_rows] + core_in[...]
+    z_ring.far()
+    z_ring.near_up()
+    z_ring.near_down()
+    d1 = diag_send(NEXT)
+    bands[0].mid_up()
+    bands[0].mid_down()
+    z_ring.mid_up()
+    z_ring.mid_down()
+    diag_take(d0, FAR)
+    diags.far()
+
+    z_sum[:, :half], z_sum[:, half:] = z_ring.end()
+    yrow = zrow // 4
+    y_copies = []
+    for d in (1, 2, 3):
+        piece = z_sum.at[pl.ds(pl.multiple_of(((y + d) % 4) * yrow, yrow), yrow)]
+        y_copies.append(net.send(piece, y_in.at[d - 1], y_peers[d - 1]))
+    d2 = diag_send(PREV)
+    bands[1].mid_up()
+    bands[1].mid_down()
+    for copy in y_copies:
+        copy.wait_recv()
+    own = z_sum[pl.ds(pl.multiple_of(y * yrow, yrow), yrow)]
+    x_all[x] = own + y_in[0] + y_in[1] + y_in[2]
+    x_copies = [net.send(x_all.at[x], x_all.at[x], peer) for peer in x_peers]
+    bands[1].near_up()
+    bands[1].near_down()
+    diag_take(d1, NEXT)
+    diags.near_up()
+    diags.mid_up()
+
+    for copy in x_copies:
+        copy.wait_recv()
+    z_rows = rows_core + z * zrow
+    y_rows = pl.ds(pl.multiple_of(z_rows + y * yrow, yrow), yrow)
+    full[y_rows] = (x_all[0] + x_all[1]) + (x_all[2] + x_all[3])
+    y_back = [net.send(full.at[y_rows], full.at[y_rows], peer) for peer in y_peers]
+    d3 = diag_send(OWN)
+    b_send[:, :half], b_send[:, half:] = bands[0].end()
+    cross = net.send(b_send, b_in, y_near)
+    diag_take(d2, PREV)
+    diags.near_down()
+    diags.mid_down()
+
+    for copy in y_back:
+        copy.wait_recv()
+
+    def z_block(offset):
+        return pl.ds(pl.multiple_of(rows_core + ((z + offset) % 4) * zrow, zrow), zrow)
+
+    mine = full.at[z_block(0)]
+    up_copy, down_copy = net.send(mine, mine, z_up), net.send(mine, mine, z_down)
+    core_backs = [net.send(mine, mine, other_core)]
+    b_keep[:, :half], b_keep[:, half:] = bands[1].end()
+    up_copy.wait_recv()
+    below = full.at[z_block(3)]
+    pass_up = net.send(full.at[z_block(3), halves[0]], full.at[z_block(3), halves[0]], z_up)
+    core_backs.append(net.send(below, below, other_core))
+    down_copy.wait_recv()
+    above = full.at[z_block(1)]
+    pass_down = net.send(full.at[z_block(1), halves[1]], full.at[z_block(1), halves[1]], z_down)
+    core_backs.append(net.send(above, above, other_core))
+    for copy in c_copies:
+        copy.wait()
+    diag_take(d3, OWN)
+    pass_up.wait_recv()
+    pass_down.wait_recv()
+    far = full.at[z_block(2)]
+    core_backs.append(net.send(far, far, other_core))
+    for h, term in enumerate(diags.end()):
+        out_d[:, :, halves[h]] = cd[:, :, halves[h]] - term
+    cross.wait_recv()
+    out_b[...] = cb[...] - (b_keep[...] + b_in[...])
+    for copy in core_backs:
+        copy.wait_recv()
+    out_f[...] = cf[...] - full[...]
+    net.drain()
+
+
+def exchange(first, band, diag, c_first, c_band, c_diag):
+    w = first.shape[0]
+    half = w // 2
+    sub, drow, k = band.shape[0] // 8, diag.shape[1] // 8, diag.shape[0]
+    zrow = half // 4
+    yrow = zrow // 4
+    vmem, hbm = pl.BlockSpec(memory_space=pltpu.VMEM), pl.BlockSpec(memory_space=pl.ANY)
+    v = lambda *shape: pltpu.VMEM(shape, F32)
+    return pl.pallas_call(
+        exchange_kernel,
+        out_shape=tuple(jax.ShapeDtypeStruct(a.shape, F32) for a in (c_first, c_band, c_diag)),
+        in_specs=[vmem] * 3 + [hbm] * 3,
+        out_specs=(vmem, vmem, vmem),
+        scratch_shapes=[
+            v(*c_first.shape), v(*c_band.shape), v(*c_diag.shape),
+            v(half, w), v(half, w), v(2, zrow, half), v(2, zrow, half), v(2, 2, zrow, half), v(zrow, w),
+            v(3, yrow, w), v(4, yrow, w), v(w, w),
+            v(2, 2, sub, half), v(2, 2, sub, half), v(2, 2, 2, sub, half), v(sub, w), v(sub, w), v(sub, w),
+            v(4, k, drow, w), v(2, k, drow, half), v(2, k, drow, half), v(2, 2, k, drow, half),
+            pltpu.SemaphoreType.DMA((64,)), pltpu.SemaphoreType.DMA((64,)), pltpu.SemaphoreType.DMA((3,)),
+        ],
+        compiler_params=pltpu.CompilerParams(
+            vmem_limit_bytes=32 << 20, collective_id=0, has_side_effects=True
+        ),
+        name="exchange",
+    )(first, band, diag, c_first, c_band, c_diag)
+
+
 def shards(counts, blocks, factors, b_first, b_branch, c_first, c_band, c_diag):
     first, band, diag = local_sums(counts, blocks, factors, b_first, b_branch, c_diag.shape[0])
-    band = band.reshape(-1, band.shape[-1])
-    band_sum = lax.psum_scatter(band, "scen", scatter_dimension=0, tiled=True)
-    diag_sum = lax.psum_scatter(diag, "scen", scatter_dimension=1, tiled=True)
-    first_sum = lax.psum(first, ("branch", "scen"))
-    return (c_first - first_sum, c_band - band_sum, c_diag - diag_sum)
+    return exchange(first, band.reshape(-1, band.shape[-1]), diag, c_first, c_band, c_diag)
 
 
 def solution(mesh):

time: 247 us -> 81.6 us (0.33)
  waiting for transfers between devices: 195 us -> 0 us
  Pallas kernels: 28.7 us -> 76.3 us
  between operations: 16.2 us -> 1.33 us
  other arithmetic: 5.78 us -> 0 us
    psum x1 -> x0, waiting for transfers between devices: 194 us -> none  [shards(): first_sum = lax.psum(first, ('branch', 'scen'))]
    pallas_call x0 -> x1, Pallas kernels: none -> 65.9 us  [exchange(): pl.pallas_call(exchange_kernel, out_shape=tuple((jax.ShapeDtypeStruct(a.s...]
    pallas_call x1, Pallas kernels: 28.7 us -> 10.3 us  [local_sums(): pl.pallas_call(compute_kernel, out_shape=(jax.ShapeDtypeStruct((w, w), F3...]
    sub x3 -> x0, other arithmetic: 5.78 us -> none  [shards(): return (c_first - first_sum, c_band - band_sum, c_diag - diag_sum)]
  transfers between devices with their start and end apart: 3 -> 0, of which waited for: 1 -> 0; matrix products, arithmetic and copies ran while one was open for 2% -> 0% of each run, Pallas kernels for 0% -> 0%
where the time goes in v2:
time: 81.6 us; the launch traced here: 80.7 us
  Pallas kernels  76.3 us (94%)
  local copies, waits for them, and re-layouts  3.04 us (4%)
  between operations  1.33 us (2%)
    pallas_call x1, Pallas kernels, exchange(): pl.pallas_call(exchange_kernel, out_shape=tuple((jax.ShapeDtypeStruct(a.s...  65.9 us
    pallas_call x1, Pallas kernels, local_sums(): pl.pallas_call(compute_kernel, out_shape=(jax.ShapeDtypeStruct((w, w), F3...  10.3 us
    unnamed x11, local copies, waits for them, and re-layouts  3.04 us

profile of v2, /device:TPU:1, one launch (start us, length us, event | category | flops | bytes accessed | tf_op | source)
XLA Modules:
  0.0 80.7 jit_solution(12606574620230448864)
XLA Ops:
  1.3 0.0 copy-start.3
  1.3 0.6 copy-done.3
  1.9 0.0 copy-start
  1.9 0.0 copy-start.1
  1.9 0.0 copy-start.2
  1.9 10.3 %local_sums.1 = (f32[512,512]{1,0:T(8,128)S(1)}, f32[2,512,512]{2,1,0:T(8,128)S(1)}, f32[2,512,512]{2,1,0:T(8,128)S(1)}) custom-call(s32[1]{0:T(128)S(6)} %copy.14.counts, s32[4]{0:T(128)S(1)} %copy-done.3, f32[4,512,512]{2,1,0:T(8,128)} %fac_hbm.1, f32[4,512,512]{2,1,0:T(8,128)} %bf_hbm.1, f32[4,512,512]{2,1,0:T(8,128)} %bb_hbm.1), custom_call_target="tpu_custom_call" | custom-call | tf_op jit(solution)/shard_map/local_sums/pallas_call | solution.py:143
  12.3 0.0 copy-done
  12.3 0.0 copy-done.1
  12.3 0.0 copy-done.2
  12.3 65.9 %exchange.1 = (f32[512,512]{1,0:T(8,128)S(1)}, f32[128,512]{1,0:T(8,128)S(1)}, f32[2,64,512]{2,1,0:T(8,128)S(1)}) custom-call(f32[512,512]{1,0:T(8,128)S(1)} %get-tuple-element.6.first, f32[1024,512]{1,0:T(8,128)S(1)} %bitcast.1, f32[2,512,512]{2,1,0:T(8,128)S(1)} %get-tuple-element.8.diag, f32[512,512]{1,0:T(8,128)S(1)} %copy-done, ...), custom_call_target="tpu_custom_call" | custom-call | tf_op jit(solution)/shard_map/exchange/pallas_call | solution.py:391
  78.3 1.0 %copy.15 = f32[512,512]{1,0:T(8,128)} copy(f32[512,512]{1,0:T(8,128)S(1)} %get-tuple-element.12) | data formatting | bytes 2097152
  79.2 0.7 copy.16
  80.0 0.7 copy.17
Async XLA Ops:
  1.3 0.7 copy-start.3
  1.9 10.4 %copy-start = (f32[512,512]{1,0:T(8,128)S(1)}, f32[512,512]{1,0:T(8,128)}, u32[]{:S(2)}) copy-start(f32[512,512]{1,0:T(8,128)} %cf_hbm.1) | copy-start | bytes 3145732
  1.9 10.4 %copy-start.1 = (f32[128,512]{1,0:T(8,128)S(1)}, f32[128,512]{1,0:T(8,128)}, u32[]{:S(2)}) copy-start(f32[128,512]{1,0:T(8,128)} %cb_hbm.1) | copy-start | bytes 786436
  1.9 10.4 %copy-start.2 = (f32[2,64,512]{2,1,0:T(8,128)S(1)}, f32[2,64,512]{2,1,0:T(8,128)}, u32[]{:S(2)}) copy-start(f32[2,64,512]{2,1,0:T(8,128)} %cd_hbm.1) | copy-start | bytes 786436

commit v3 on v2

--- a/solution.py
+++ b/solution.py
@@ -28,6 +28,10 @@
     left = lane < wide.shape[0]
     zero = jnp.zeros_like(wide)
     return jnp.concatenate([jnp.where(left, wide, zero), jnp.where(left, zero, wide)], axis=0)
+
+
+def dot1(left, right):
+    return lax.dot_general(left.astype(BF16), right.astype(BF16), (NN, ((), ())), preferred_element_type=F32)
 
 
 def pair_inverses(wides):
@@ -51,76 +55,95 @@
     shift = 1
     while (1 << shift) < rows:
         below = ((r >> (shift + 1)) == (c >> (shift + 1))) & ((r >> shift) > (c >> shift))
-        inv = [split(x) for x in out]
-        inv_on = [split(on_diagonal(x)) for x in out]
-        mid = [dot3(split(jnp.where(below, w, 0.0)), x, NN) for w, x in zip(wides, inv_on)]
-        mid_on = [split(on_diagonal(m)) for m in mid]
-        out = [x - dot3(xs, m, NN) for x, xs, m in zip(out, inv, mid_on)]
+        mids = [dot1(jnp.where(below, w, 0.0), on_diagonal(x)) for w, x in zip(wides, out)]
+        out = [x - dot1(x, on_diagonal(m)) for x, m in zip(out, mids)]
         shift += 1
+    unit = jnp.where(eye, 1.0, 0.0)
+    for _ in range(NEWTON):
+        errs = [unit - dot3(split(w), split(on_diagonal(x)), NN) for w, x in zip(wides, out)]
+        out = [x + dot1(x, on_diagonal(e)) for x, e in zip(out, errs)]
     return out
 
 
-def half_inverses(factor, half):
-    q = half // 2
+NEWTON = 2
+
+
+def invert(fac, inv_h, inv_l, slots):
+    n = fac.shape[1]
+    half, q = n // 2, n // 4
     wides = []
-    for start in (0, half):
-        a = factor[start : start + q, start : start + q]
-        d = factor[start + q : start + half, start + q : start + half]
-        wides.append(jnp.concatenate([a, d], axis=1))
+    for s in slots:
+        for o in (0, half):
+            wides.append(
+                jnp.concatenate([fac[s, o : o + q, o : o + q], fac[s, o + q : o + half, o + q : o + half]], axis=1)
+            )
     invs = pair_inverses(wides)
-    full = []
-    for start, wide in zip((0, half), invs):
-        a, d = split(wide[:, :q]), split(wide[:, q:])
-        low = split(factor[start + q : start + half, start : start + q])
-        corner = -dot3(d, split(dot3(low, a, NN)), NN)
-        top = jnp.concatenate([wide[:, :q], jnp.zeros((q, q), F32)], axis=1)
-        full.append(jnp.concatenate([top, jnp.concatenate([corner, wide[:, q:]], axis=1)], axis=0))
-    return full
-
-
-def compute_kernel(counts, blocks, fac_hbm, bf_hbm, bb_hbm, first, band, diag, fac, rhs, yh, yl, sems):
+    parts = [(split(w[:, :q]), split(w[:, q:])) for w in invs]
+    lows = [
+        dot3(split(fac[s, o + q : o + half, o : o + q]), parts[2 * i + j][0], NN)
+        for i, s in enumerate(slots)
+        for j, o in enumerate((0, half))
+    ]
+    corners = [split(-dot3(p[1], split(m), NN)) for p, m in zip(parts, lows)]
+    zero = jnp.zeros((q, q), BF16)
+    for i, s in enumerate(slots):
+        for j, o in enumerate((0, half)):
+            (a, d), corner = parts[2 * i + j], corners[2 * i + j]
+            for h, ref in enumerate((inv_h, inv_l)):
+                ref[s, o : o + q, o : o + q] = a[h]
+                ref[s, o : o + q, o + q : o + half] = zero
+                ref[s, o + q : o + half, o : o + q] = corner[h]
+                ref[s, o + q : o + half, o + q : o + half] = d[h]
+    lows = [
+        dot3(split(fac[s, half:, :half]), (inv_h[s, :half, :half], inv_l[s, :half, :half]), NN) for s in slots
+    ]
+    for s, low in zip(slots, lows):
+        corner = -dot3((inv_h[s, half:, half:], inv_l[s, half:, half:]), split(low), NN)
+        inv_h[s, half:, :half], inv_l[s, half:, :half] = split(corner)
+
+
+def compute_kernel(counts, blocks, fac_hbm, bf_hbm, bb_hbm, first, band, diag, fac, rhs, inv_h, inv_l, yh, yl, sems):
     n, w = fac_hbm.shape[1], bf_hbm.shape[2]
+    cap = fac_hbm.shape[0]
     half = n // 2
     live = counts[0]
-
-    def loads(s):
-        return (
-            pltpu.make_async_copy(fac_hbm.at[s], fac.at[s], sems.at[s, 0]),
+    fac_loads = [pltpu.make_async_copy(fac_hbm.at[s], fac.at[s], sems.at[s, 0]) for s in range(cap)]
+    rhs_loads = [
+        (
             pltpu.make_async_copy(bf_hbm.at[s], rhs.at[s, :, pl.ds(0, w)], sems.at[s, 1]),
             pltpu.make_async_copy(bb_hbm.at[s], rhs.at[s, :, pl.ds(w, w)], sems.at[s, 2]),
         )
-
-    @pl.loop(0, live)
-    def _(s):
-        for copy in loads(s):
+        for s in range(cap)
+    ]
+    for copy in fac_loads:
+        copy.start()
+    for pair in rhs_loads:
+        for copy in pair:
             copy.start()
-
     first[...] = jnp.zeros_like(first)
     band[...] = jnp.zeros_like(band)
     diag[...] = jnp.zeros_like(diag)
+    for copy in fac_loads:
+        copy.wait()
+    for g in range(0, cap, GROUP):
+        invert(fac, inv_h, inv_l, range(g, g + GROUP))
+    for pair in rhs_loads:
+        for copy in pair:
+            copy.wait()
 
     @pl.loop(0, live)
     def _(s):
-        load_f, load_a, load_b = loads(s)
-        load_f.wait()
-        factor = fac.at[s]
-        inv_top, inv_low = (split(x) for x in half_inverses(factor, half))
-        link = split(factor[half:, :half])
-        load_a.wait()
-        load_b.wait()
+        top = (inv_h[s, :half, :half], inv_l[s, :half, :half])
+        low = (inv_h[s, half:, :], inv_l[s, half:, :])
         for col in range(0, 2 * w, half):
             cols = pl.ds(col, half)
-            top = dot3(inv_top, split(rhs[s, :half, cols]), NN)
-            top_s = split(top)
-            yh[:half, cols], yl[:half, cols] = top_s
-            low = dot3(inv_low, split(rhs[s, half:, cols] - dot3(link, top_s, NN)), NN)
-            yh[half:, cols], yl[half:, cols] = split(low)
+            right = split(rhs[s, :, cols])
+            yh[:half, cols], yl[:half, cols] = split(dot3(top, (right[0][:half], right[1][:half]), NN))
+            yh[half:, cols], yl[half:, cols] = split(dot3(low, right, NN))
         k = blocks[s] & 1
         for i in range(0, 2 * w, half):
             left = (yh[:, pl.ds(i, half)], yl[:, pl.ds(i, half)])
             for j in range(0, i + half, half):
-                if i >= w and j >= w and j > i:
-                    continue
                 right = (yh[:, pl.ds(j, half)], yl[:, pl.ds(j, half)])
                 term = dot3(left, right, TN)
                 if i < w:
@@ -133,6 +156,9 @@
     first[:half, half:] = first[half:, :half].T
     for k in range(diag.shape[0]):
         diag[k, :half, half:] = diag[k, half:, :half].T
+
+
+GROUP = 4
 
 
 def local_sums(counts, blocks, factors, b_first, b_branch, block_count):
@@ -152,6 +178,8 @@
         scratch_shapes=[
             pltpu.VMEM((cap, n, n), F32),
             pltpu.VMEM((cap, n, 2 * w), F32),
+            pltpu.VMEM((cap, n, n), BF16),
+            pltpu.VMEM((cap, n, n), BF16),
             pltpu.VMEM((n, 2 * w), BF16),
             pltpu.VMEM((n, 2 * w), BF16),
             pltpu.SemaphoreType.DMA((cap, 3)),

time: 81.6 us -> 69.9 us (0.86); the launches traced: 80.7 us -> 70.8 us
  Pallas kernels: 76.3 us -> 66.4 us
    pallas_call x1, Pallas kernels: 65.9 us -> 43.9 us  [exchange(): pl.pallas_call(exchange_kernel, out_shape=tuple((jax.ShapeDtypeStruct(a.s...]
    pallas_call x1, Pallas kernels: 10.3 us -> 22.5 us  [local_sums(): pl.pallas_call(compute_kernel, out_shape=(jax.ShapeDtypeStruct((w, w), F3...]
where the time goes in v3:
time: 69.9 us; the launch traced here: 70.8 us
  Pallas kernels  66.4 us (95%)
  local copies, waits for them, and re-layouts  3.04 us (4%)
  between operations  1.33 us (2%)
    pallas_call x1, Pallas kernels, exchange(): pl.pallas_call(exchange_kernel, out_shape=tuple((jax.ShapeDtypeStruct(a.s...  43.9 us
    pallas_call x1, Pallas kernels, local_sums(): pl.pallas_call(compute_kernel, out_shape=(jax.ShapeDtypeStruct((w, w), F3...  22.5 us
    unnamed x11, local copies, waits for them, and re-layouts  3.04 us

profile of v3, /device:TPU:1, one launch (start us, length us, event | category | flops | bytes accessed | tf_op | source)
XLA Modules:
  0.0 70.8 jit_solution(6359618341552605529)
XLA Ops:
  1.3 0.0 copy-start.3
  1.3 0.6 copy-done.3
  1.9 0.0 copy-start
  1.9 0.0 copy-start.1
  1.9 0.0 copy-start.2
  1.9 22.5 %local_sums.1 = (f32[512,512]{1,0:T(8,128)S(1)}, f32[2,512,512]{2,1,0:T(8,128)S(1)}, f32[2,512,512]{2,1,0:T(8,128)S(1)}) custom-call(s32[1]{0:T(128)S(6)} %copy.14.counts, s32[4]{0:T(128)S(1)} %copy-done.3, f32[4,512,512]{2,1,0:T(8,128)} %fac_hbm.1, f32[4,512,512]{2,1,0:T(8,128)} %bf_hbm.1, f32[4,512,512]{2,1,0:T(8,128)} %bb_hbm.1), custom_call_target="tpu_custom_call" | custom-call | tf_op jit(solution)/shard_map/local_sums/pallas_call | solution.py:169
  24.4 0.0 copy-done
  24.5 0.0 copy-done.1
  24.5 0.0 copy-done.2
  24.5 43.9 %exchange.1 = (f32[512,512]{1,0:T(8,128)S(1)}, f32[128,512]{1,0:T(8,128)S(1)}, f32[2,64,512]{2,1,0:T(8,128)S(1)}) custom-call(f32[512,512]{1,0:T(8,128)S(1)} %get-tuple-element.6.first, f32[1024,512]{1,0:T(8,128)S(1)} %bitcast.1, f32[2,512,512]{2,1,0:T(8,128)S(1)} %get-tuple-element.8.diag, f32[512,512]{1,0:T(8,128)S(1)} %copy-done, ...), custom_call_target="tpu_custom_call" | custom-call | tf_op jit(solution)/shard_map/exchange/pallas_call | solution.py:419
  68.4 1.0 %copy.15 = f32[512,512]{1,0:T(8,128)} copy(f32[512,512]{1,0:T(8,128)S(1)} %get-tuple-element.12) | data formatting | bytes 2097152
  69.4 0.7 copy.16
  70.1 0.7 copy.17
Async XLA Ops:
  1.3 0.7 copy-start.3
  1.9 22.5 %copy-start = (f32[512,512]{1,0:T(8,128)S(1)}, f32[512,512]{1,0:T(8,128)}, u32[]{:S(2)}) copy-start(f32[512,512]{1,0:T(8,128)} %cf_hbm.1) | copy-start | bytes 3145732
  1.9 22.5 %copy-start.1 = (f32[128,512]{1,0:T(8,128)S(1)}, f32[128,512]{1,0:T(8,128)}, u32[]{:S(2)}) copy-start(f32[128,512]{1,0:T(8,128)} %cb_hbm.1) | copy-start | bytes 786436
  1.9 22.5 %copy-start.2 = (f32[2,64,512]{2,1,0:T(8,128)S(1)}, f32[2,64,512]{2,1,0:T(8,128)}, u32[]{:S(2)}) copy-start(f32[2,64,512]{2,1,0:T(8,128)} %cd_hbm.1) | copy-start | bytes 786436

commit v4 on v3

--- a/solution.py
+++ b/solution.py
@@ -102,93 +102,6 @@
         inv_h[s, half:, :half], inv_l[s, half:, :half] = split(corner)
 
 
-def compute_kernel(counts, blocks, fac_hbm, bf_hbm, bb_hbm, first, band, diag, fac, rhs, inv_h, inv_l, yh, yl, sems):
-    n, w = fac_hbm.shape[1], bf_hbm.shape[2]
-    cap = fac_hbm.shape[0]
-    half = n // 2
-    live = counts[0]
-    fac_loads = [pltpu.make_async_copy(fac_hbm.at[s], fac.at[s], sems.at[s, 0]) for s in range(cap)]
-    rhs_loads = [
-        (
-            pltpu.make_async_copy(bf_hbm.at[s], rhs.at[s, :, pl.ds(0, w)], sems.at[s, 1]),
-            pltpu.make_async_copy(bb_hbm.at[s], rhs.at[s, :, pl.ds(w, w)], sems.at[s, 2]),
-        )
-        for s in range(cap)
-    ]
-    for copy in fac_loads:
-        copy.start()
-    for pair in rhs_loads:
-        for copy in pair:
-            copy.start()
-    first[...] = jnp.zeros_like(first)
-    band[...] = jnp.zeros_like(band)
-    diag[...] = jnp.zeros_like(diag)
-    for copy in fac_loads:
-        copy.wait()
-    for g in range(0, cap, GROUP):
-        invert(fac, inv_h, inv_l, range(g, g + GROUP))
-    for pair in rhs_loads:
-        for copy in pair:
-            copy.wait()
-
-    @pl.loop(0, live)
-    def _(s):
-        top = (inv_h[s, :half, :half], inv_l[s, :half, :half])
-        low = (inv_h[s, half:, :], inv_l[s, half:, :])
-        for col in range(0, 2 * w, half):
-            cols = pl.ds(col, half)
-            right = split(rhs[s, :, cols])
-            yh[:half, cols], yl[:half, cols] = split(dot3(top, (right[0][:half], right[1][:half]), NN))
-            yh[half:, cols], yl[half:, cols] = split(dot3(low, right, NN))
-        k = blocks[s] & 1
-        for i in range(0, 2 * w, half):
-            left = (yh[:, pl.ds(i, half)], yl[:, pl.ds(i, half)])
-            for j in range(0, i + half, half):
-                right = (yh[:, pl.ds(j, half)], yl[:, pl.ds(j, half)])
-                term = dot3(left, right, TN)
-                if i < w:
-                    first[pl.ds(i, half), pl.ds(j, half)] += term
-                elif j < w:
-                    band[k, pl.ds(i - w, half), pl.ds(j, half)] += term
-                else:
-                    diag[k, pl.ds(i - w, half), pl.ds(j - w, half)] += term
-
-    first[:half, half:] = first[half:, :half].T
-    for k in range(diag.shape[0]):
-        diag[k, :half, half:] = diag[k, half:, :half].T
-
-
-GROUP = 4
-
-
-def local_sums(counts, blocks, factors, b_first, b_branch, block_count):
-    cap, n, w = b_first.shape
-    smem = pl.BlockSpec(memory_space=pltpu.SMEM)
-    hbm = pl.BlockSpec(memory_space=pl.ANY)
-    vmem = pl.BlockSpec(memory_space=pltpu.VMEM)
-    return pl.pallas_call(
-        compute_kernel,
-        out_shape=(
-            jax.ShapeDtypeStruct((w, w), F32),
-            jax.ShapeDtypeStruct((block_count, w, w), F32),
-            jax.ShapeDtypeStruct((block_count, w, w), F32),
-        ),
-        in_specs=[smem, smem, hbm, hbm, hbm],
-        out_specs=(vmem, vmem, vmem),
-        scratch_shapes=[
-            pltpu.VMEM((cap, n, n), F32),
-            pltpu.VMEM((cap, n, 2 * w), F32),
-            pltpu.VMEM((cap, n, n), BF16),
-            pltpu.VMEM((cap, n, n), BF16),
-            pltpu.VMEM((n, 2 * w), BF16),
-            pltpu.VMEM((n, 2 * w), BF16),
-            pltpu.SemaphoreType.DMA((cap, 3)),
-        ],
-        compiler_params=pltpu.CompilerParams(vmem_limit_bytes=48 << 20),
-        name="local_sums",
-    )(counts, blocks, factors, b_first, b_branch)
-
-
 class Net:
     def __init__(self, send_sems, recv_sems):
         self.sems = (send_sems, recv_sems)
@@ -249,19 +162,30 @@
         return [self.piece(OWN, h)[...] + self.near_in[0, h] + self.near_in[1, h] for h in range(2)]
 
 
-def exchange_kernel(
-    first, band, diag, cf_hbm, cb_hbm, cd_hbm, out_f, out_b, out_d,
-    cf, cb, cd, core_in, held, z_far, z_out, z_near, z_sum, y_in, x_all, full,
-    b_far, b_out, b_near, b_send, b_in, b_keep, d_in, d_far, d_out, d_near, send_sems, recv_sems, c_sems,
+def fused_kernel(
+    counts, blocks, fac_hbm, bf_hbm, bb_hbm, out_f, out_b, out_d,
+    fac, rhs, inv_h, inv_l, y0_h, y0_l, y1_h, y1_l, first, band, diag,
+    core_in, held, z_far, z_out, z_near, z_sum, y_in, x_all, full,
+    b_far, b_out, b_near, b_send, b_in, b_keep, d_in, d_far, d_out, d_near,
+    load_sems, send_sems, recv_sems,
 ):
     b, s = lax.axis_index("branch"), lax.axis_index("scen")
     z, y_hi, core = b // 4, (b // 2) % 2, b % 2
     x, y_lo = s // 2, s % 2
     y = 2 * y_hi + y_lo
-    w = first.shape[1]
+    cap, n, w = bf_hbm.shape
     half = w // 2
     halves = (pl.ds(0, half), pl.ds(half, half))
     net = Net(send_sems, recv_sems)
+
+    fac_loads = [pltpu.make_async_copy(fac_hbm.at[t], fac.at[t], load_sems.at[t]) for t in range(cap)]
+    rest = []
+    for t in range(cap):
+        rest.append((bf_hbm.at[t], rhs.at[t, :, pl.ds(0, w)]))
+        rest.append((bb_hbm.at[t], rhs.at[t, :, pl.ds(w, w)]))
+    rest_loads = [pltpu.make_async_copy(a, c, load_sems.at[cap + i]) for i, (a, c) in enumerate(rest)]
+    for copy in fac_loads + rest_loads:
+        copy.start()
 
     other_core = (b + 1 - 2 * core, s)
     z_up, z_down = (((z + 1) % 4) * 4 + b % 4, s), (((z + 3) % 4) * 4 + b % 4, s)
@@ -272,45 +196,104 @@
     x_peers = [(b, ((x + d) % 4) * 2 + y_lo) for d in (1, 2, 3)]
     x_up, x_down = x_peers[0], x_peers[2]
     y_near = (b, x * 2 + 1 - y_lo)
-
-    c_copies = [
-        pltpu.make_async_copy(source, target, c_sems.at[i])
-        for i, (source, target) in enumerate(((cf_hbm, cf), (cb_hbm, cb), (cd_hbm, cd)))
-    ]
-    for copy in c_copies:
-        copy.start()
-
     barrier = pltpu.get_barrier_semaphore()
     greeted = [other_core, z_up, z_down] + y_peers + x_peers
     for peer in greeted:
         pl.semaphore_signal(barrier, inc=1, device_id=peer, device_id_type=pl.DeviceIdType.MESH)
+
+    for copy in fac_loads:
+        copy.wait()
+    invert(fac, inv_h, inv_l, range(cap))
+    for copy in rest_loads:
+        copy.wait()
+
+    first[...] = jnp.zeros_like(first)
+
+    def chosen(t, shape):
+        return jnp.broadcast_to(jnp.where(t < counts[0], blocks[t] % 2, 2), shape)
+
+    def solve(t, start, y_h, y_l):
+        top = (inv_h[t, :half, :half], inv_l[t, :half, :half])
+        low = (inv_h[t, half:, :], inv_l[t, half:, :])
+        live = chosen(t, (half, half)) < 2
+        for cols in halves:
+            right = split(rhs[t, :, pl.ds(start + cols.start, half)])
+            up = dot3(top, (right[0][:half], right[1][:half]), NN)
+            y_h[t, :half, cols], y_l[t, :half, cols] = split(jnp.where(live, up, 0.0))
+            down = dot3(low, right, NN)
+            y_h[t, half:, cols], y_l[t, half:, cols] = split(jnp.where(live, down, 0.0))
+
+    @pl.loop(0, cap)
+    def _(t):
+        solve(t, 0, y0_h, y0_l)
+        for i in range(0, w, half):
+            left = (y0_h[t, :, pl.ds(i, half)], y0_l[t, :, pl.ds(i, half)])
+            for j in range(0, i + half, half):
+                right = (y0_h[t, :, pl.ds(j, half)], y0_l[t, :, pl.ds(j, half)])
+                first[pl.ds(i, half), pl.ds(j, half)] += dot3(left, right, TN)
+
+    first[:half, half:] = first[half:, :half].T
+
     pl.semaphore_wait(barrier, len(greeted))
-
     rows_core = pl.multiple_of(core * half, half)
     core_rows, core_far = pl.ds(rows_core, half), pl.ds(pl.multiple_of((1 - core) * half, half), half)
     core_copy = net.send(first.at[core_far], core_in, other_core)
 
-    sub = band.shape[0] // 8
+    @pl.loop(0, cap)
+    def _(t):
+        solve(t, w, y1_h, y1_l)
+
+    quarter = half // 2
+
+    def place(role):
+        return (x + OFFSETS[role]) % 4
+
+    def band_terms(pair):
+        cols = pl.ds(pl.multiple_of((place(pair[0]) % 2) * half, half), half)
+        for role in pair:
+            band[role] = jnp.zeros((half, w), F32)
+
+        @pl.loop(0, cap)
+        def _(t):
+            which = chosen(t, (half, w))
+            term = dot3((y1_h[t, :, cols], y1_l[t, :, cols]), (y0_h[t], y0_l[t]), TN)
+            for role in pair:
+                band[role] += jnp.where(which == place(role) // 2, term, 0.0)
+
+    def diag_terms(pair):
+        cols = [pl.ds(pl.multiple_of(place(role) * quarter, quarter), quarter) for role in pair]
+        for role in pair:
+            diag[role] = jnp.zeros((half, w), F32)
+
+        @pl.loop(0, cap)
+        def _(t):
+            which = chosen(t, (quarter, w))
+            left = [jnp.concatenate([y[t, :, c] for c in cols], axis=1) for y in (y1_h, y1_l)]
+            term = dot3(left, (y1_h[t], y1_l[t]), TN)
+            for i, role in enumerate(pair):
+                for k in range(2):
+                    part = jnp.where(which == k, term[i * quarter : (i + 1) * quarter], 0.0)
+                    diag[role, pl.ds(k * quarter, quarter)] += part
+
+    sub, drow = half // 2, quarter // 2
     bands = []
     for chunk, y_to in enumerate((1 - y_lo, y_lo)):
 
         def band_piece(role, h, y_to=y_to):
-            start = ((x + OFFSETS[role]) % 4) * (2 * sub) + y_to * sub
-            return band.at[pl.ds(pl.multiple_of(start, sub), sub), halves[h]]
+            return band.at[role, pl.ds(pl.multiple_of(y_to * sub, sub), sub), halves[h]]
 
         bands.append(Ring(net, band_piece, x_up, x_down, b_far.at[chunk], b_out.at[chunk], b_near.at[chunk]))
-    drow = diag.shape[1] // 8
-
-    def diag_rows(role, y_to):
-        start = ((x + OFFSETS[role]) % 4) * (2 * drow) + y_to * drow
-        return diag.at[:, pl.ds(pl.multiple_of(start, drow), drow), :]
+
+    def diag_rows(role, k, y_to):
+        return diag.at[role, pl.ds(pl.multiple_of(k * quarter + y_to * drow, drow), drow), :]
 
     def diag_send(role):
-        return net.send(diag_rows(role, 1 - y_lo), d_in.at[role], y_near)
-
-    def diag_take(copy, role):
-        copy.wait_recv()
-        d_in[role] += diag_rows(role, y_lo)[...]
+        return [net.send(diag_rows(role, k, 1 - y_lo), d_in.at[role, k], y_near) for k in range(2)]
+
+    def diag_take(copies, role):
+        for k, copy in enumerate(copies):
+            copy.wait_recv()
+            d_in[role, k] += diag_rows(role, k, y_lo)[...]
 
     diags = Ring(net, lambda role, h: d_in.at[role, :, :, halves[h]], x_up, x_down, d_far, d_out, d_near)
 
@@ -321,45 +304,41 @@
         z_up, z_down, z_far, z_out, z_near,
     )
 
-    bands[0].far()
-    d0 = diag_send(FAR)
-    bands[1].far()
-    bands[0].near_up()
-    bands[0].near_down()
-
     core_copy.wait_recv()
     held[...] = first[core_rows] + core_in[...]
     z_ring.far()
     z_ring.near_up()
     z_ring.near_down()
-    d1 = diag_send(NEXT)
-    bands[0].mid_up()
-    bands[0].mid_down()
+    diag_terms((FAR, OWN))
+    d0 = diag_send(FAR)
     z_ring.mid_up()
     z_ring.mid_down()
-    diag_take(d0, FAR)
-    diags.far()
-
+    band_terms((FAR, OWN))
+    bands[0].far()
+    bands[1].far()
+    diag_terms((NEXT, PREV))
     z_sum[:, :half], z_sum[:, half:] = z_ring.end()
     yrow = zrow // 4
     y_copies = []
     for d in (1, 2, 3):
         piece = z_sum.at[pl.ds(pl.multiple_of(((y + d) % 4) * yrow, yrow), yrow)]
         y_copies.append(net.send(piece, y_in.at[d - 1], y_peers[d - 1]))
-    d2 = diag_send(PREV)
-    bands[1].mid_up()
-    bands[1].mid_down()
+    d1 = diag_send(NEXT)
+    band_terms((NEXT, PREV))
+    bands[0].near_up()
+    bands[0].near_down()
     for copy in y_copies:
         copy.wait_recv()
     own = z_sum[pl.ds(pl.multiple_of(y * yrow, yrow), yrow)]
     x_all[x] = own + y_in[0] + y_in[1] + y_in[2]
     x_copies = [net.send(x_all.at[x], x_all.at[x], peer) for peer in x_peers]
+    d2 = diag_send(PREV)
+    bands[0].mid_up()
+    bands[0].mid_down()
+    diag_take(d0, FAR)
+    diags.far()
     bands[1].near_up()
     bands[1].near_down()
-    diag_take(d1, NEXT)
-    diags.near_up()
-    diags.mid_up()
-
     for copy in x_copies:
         copy.wait_recv()
     z_rows = rows_core + z * zrow
@@ -367,6 +346,11 @@
     full[y_rows] = (x_all[0] + x_all[1]) + (x_all[2] + x_all[3])
     y_back = [net.send(full.at[y_rows], full.at[y_rows], peer) for peer in y_peers]
     d3 = diag_send(OWN)
+    bands[1].mid_up()
+    bands[1].mid_down()
+    diag_take(d1, NEXT)
+    diags.near_up()
+    diags.mid_up()
     b_send[:, :half], b_send[:, half:] = bands[0].end()
     cross = net.send(b_send, b_in, y_near)
     diag_take(d2, PREV)
@@ -391,54 +375,59 @@
     above = full.at[z_block(1)]
     pass_down = net.send(full.at[z_block(1), halves[1]], full.at[z_block(1), halves[1]], z_down)
     core_backs.append(net.send(above, above, other_core))
-    for copy in c_copies:
-        copy.wait()
     diag_take(d3, OWN)
     pass_up.wait_recv()
     pass_down.wait_recv()
     far = full.at[z_block(2)]
     core_backs.append(net.send(far, far, other_core))
     for h, term in enumerate(diags.end()):
-        out_d[:, :, halves[h]] = cd[:, :, halves[h]] - term
+        out_d[:, :, halves[h]] = term
     cross.wait_recv()
-    out_b[...] = cb[...] - (b_keep[...] + b_in[...])
+    out_b[...] = b_keep[...] + b_in[...]
     for copy in core_backs:
         copy.wait_recv()
-    out_f[...] = cf[...] - full[...]
+    out_f[...] = full[...]
     net.drain()
 
 
-def exchange(first, band, diag, c_first, c_band, c_diag):
-    w = first.shape[0]
+def fused(counts, blocks, factors, b_first, b_branch, c_first, c_band, c_diag):
+    cap, n, w = b_first.shape
     half = w // 2
-    sub, drow, k = band.shape[0] // 8, diag.shape[1] // 8, diag.shape[0]
+    k, drow = c_diag.shape[0], c_diag.shape[1]
+    sub = c_band.shape[0]
     zrow = half // 4
     yrow = zrow // 4
-    vmem, hbm = pl.BlockSpec(memory_space=pltpu.VMEM), pl.BlockSpec(memory_space=pl.ANY)
+    smem, vmem = pl.BlockSpec(memory_space=pltpu.SMEM), pl.BlockSpec(memory_space=pltpu.VMEM)
+    hbm = pl.BlockSpec(memory_space=HBM)
     v = lambda *shape: pltpu.VMEM(shape, F32)
+    vb = lambda *shape: pltpu.VMEM(shape, BF16)
     return pl.pallas_call(
-        exchange_kernel,
+        fused_kernel,
         out_shape=tuple(jax.ShapeDtypeStruct(a.shape, F32) for a in (c_first, c_band, c_diag)),
-        in_specs=[vmem] * 3 + [hbm] * 3,
+        in_specs=[smem] * 2 + [hbm] * 3,
         out_specs=(vmem, vmem, vmem),
         scratch_shapes=[
-            v(*c_first.shape), v(*c_band.shape), v(*c_diag.shape),
+            v(cap, n, n), v(cap, n, 2 * w), vb(cap, n, n), vb(cap, n, n),
+            vb(cap, n, w), vb(cap, n, w), vb(cap, n, w), vb(cap, n, w),
+            v(w, w), v(4, half, w), v(4, half, w),
             v(half, w), v(half, w), v(2, zrow, half), v(2, zrow, half), v(2, 2, zrow, half), v(zrow, w),
             v(3, yrow, w), v(4, yrow, w), v(w, w),
             v(2, 2, sub, half), v(2, 2, sub, half), v(2, 2, 2, sub, half), v(sub, w), v(sub, w), v(sub, w),
             v(4, k, drow, w), v(2, k, drow, half), v(2, k, drow, half), v(2, 2, k, drow, half),
-            pltpu.SemaphoreType.DMA((64,)), pltpu.SemaphoreType.DMA((64,)), pltpu.SemaphoreType.DMA((3,)),
+            pltpu.SemaphoreType.DMA((3 * cap,)),
+            pltpu.SemaphoreType.DMA((64,)), pltpu.SemaphoreType.DMA((64,)),
         ],
-        compiler_params=pltpu.CompilerParams(
-            vmem_limit_bytes=32 << 20, collective_id=0, has_side_effects=True
-        ),
-        name="exchange",
-    )(first, band, diag, c_first, c_band, c_diag)
+        compiler_params=pltpu.CompilerParams(vmem_limit_bytes=46 << 20, collective_id=0, has_side_effects=True),
+        name="schur",
+    )(counts, blocks, factors, b_first, b_branch)
+
+
+HBM = pltpu.HBM
 
 
 def shards(counts, blocks, factors, b_first, b_branch, c_first, c_band, c_diag):
-    first, band, diag = local_sums(counts, blocks, factors, b_first, b_branch, c_diag.shape[0])
-    return exchange(first, band.reshape(-1, band.shape[-1]), diag, c_first, c_band, c_diag)
+    first, band, diag = fused(counts, blocks, factors, b_first, b_branch, c_first, c_band, c_diag)
+    return c_first - first, c_band - band, c_diag - diag
 
 
 def solution(mesh):

time: 69.9 us -> 65.2 us (0.933); the launches traced: 70.8 us -> 65 us
  Pallas kernels: 66.4 us -> 58.2 us
  other arithmetic: 0 us -> 2.65 us
    pallas_call x2 -> x1, Pallas kernels: 66.4 us -> 58.2 us  [fused(): pl.pallas_call(fused_kernel, out_shape=tuple((jax.ShapeDtypeStruct(a.shap...]
    sub x0 -> x3, other arithmetic: none -> 2.65 us  [shards(): return (c_first - first, c_band - band, c_diag - diag)]
    unnamed x11 -> x10, local copies, waits for them, and re-layouts: 3.04 us -> 2.85 us
where the time goes in v4:
time: 65.2 us; the launch traced here: 65 us
  Pallas kernels  58.2 us (89%)
  local copies, waits for them, and re-layouts  2.85 us (4%)
  other arithmetic  2.65 us (4%)
  between operations  1.31 us (2%)
    pallas_call x1, Pallas kernels, fused(): pl.pallas_call(fused_kernel, out_shape=tuple((jax.ShapeDtypeStruct(a.shap...  58.2 us
    unnamed x10, local copies, waits for them, and re-layouts  2.85 us
    sub x3, other arithmetic, shards(): return (c_first - first, c_band - band, c_diag - diag)  2.65 us

profile of v4, /device:TPU:1, one launch (start us, length us, event | category | flops | bytes accessed | tf_op | source)
XLA Modules:
  0.0 65.0 jit_solution(9686163618339174161)
XLA Ops:
  1.3 0.0 copy-start
  1.3 2.2 %copy-done = f32[4,512,512]{2,1,0:T(8,128)S(1)} copy-done((f32[4,512,512]{2,1,0:T(8,128)S(1)}, f32[4,512,512]{2,1,0:T(8,128)}, u32[]{:S(2)}) %copy-start) | copy-done | bytes 4194328
  3.5 0.0 copy-start.1
  3.5 0.7 %copy-done.1 = s32[4]{0:T(128)S(1)} copy-done((s32[4]{0:T(128)S(1)}, s32[4]{0:T(128)}, u32[]{:S(2)}) %copy-start.1) | copy-done | bytes 40
  4.1 0.0 copy-start.2
  4.1 0.0 copy-start.3
  4.1 0.0 copy-start.4
  4.1 58.2 %schur.1 = (f32[512,512]{1,0:T(8,128)S(1)}, f32[128,512]{1,0:T(8,128)S(1)}, f32[2,64,512]{2,1,0:T(8,128)S(1)}) custom-call(s32[1]{0:T(128)S(6)} %copy.11.counts, s32[4]{0:T(128)S(1)} %copy-done.1, f32[4,512,512]{2,1,0:T(8,128)S(1)} %copy-done, f32[4,512,512]{2,1,0:T(8,128)} %bf_hbm.1, f32[4,512,512]{2,1,0:T(8,128)} %bb_hbm.1), custom_call_target="tpu_custom_call" | custom-call | tf_op jit(solution)/shard_map/schur/pallas_call | solution.py:404
  62.4 0.0 copy-done.2
  62.4 1.2 %sub.9 = f32[512,512]{1,0:T(8,128)} subtract(f32[512,512]{1,0:T(8,128)S(1)} %copy-done.2, f32[512,512]{1,0:T(8,128)S(1)} %get-tuple-element.6) | non-fusion elementwise | flops 262144 | bytes 3145728 | tf_op jit(solution)/shard_map/sub | solution.py:430
  63.6 0.0 copy-done.3
  63.6 0.7 %sub.10 = f32[128,512]{1,0:T(8,128)} subtract(f32[128,512]{1,0:T(8,128)S(1)} %copy-done.3, f32[128,512]{1,0:T(8,128)S(1)} %get-tuple-element.7) | non-fusion elementwise | flops 65536 | bytes 786432 | tf_op jit(solution)/shard_map/sub | solution.py:430
  64.3 0.0 copy-done.4
  64.3 0.7 %sub.11 = f32[2,64,512]{2,1,0:T(8,128)} subtract(f32[2,64,512]{2,1,0:T(8,128)S(1)} %copy-done.4, f32[2,64,512]{2,1,0:T(8,128)S(1)} %get-tuple-element.8) | non-fusion elementwise | flops 65536 | bytes 786432 | tf_op jit(solution)/shard_map/sub | solution.py:430
Async XLA Ops:
  1.3 2.2 %copy-start = (f32[4,512,512]{2,1,0:T(8,128)S(1)}, f32[4,512,512]{2,1,0:T(8,128)}, u32[]{:S(2)}) copy-start(f32[4,512,512]{2,1,0:T(8,128)} %fac_hbm.1) | copy-start | bytes 12582916
  3.5 0.7 %copy-start.1 = (s32[4]{0:T(128)S(1)}, s32[4]{0:T(128)}, u32[]{:S(2)}) copy-start(s32[4]{0:T(128)} %blocks.1) | copy-start | bytes 52
  4.1 58.3 %copy-start.2 = (f32[512,512]{1,0:T(8,128)S(1)}, f32[512,512]{1,0:T(8,128)}, u32[]{:S(2)}) copy-start(f32[512,512]{1,0:T(8,128)} %param.13) | copy-start | bytes 3145732
  4.1 59.4 %copy-start.3 = (f32[128,512]{1,0:T(8,128)S(1)}, f32[128,512]{1,0:T(8,128)}, u32[]{:S(2)}) copy-start(f32[128,512]{1,0:T(8,128)} %param.14) | copy-start | bytes 786436
  4.1 60.2 %copy-start.4 = (f32[2,64,512]{2,1,0:T(8,128)S(1)}, f32[2,64,512]{2,1,0:T(8,128)}, u32[]{:S(2)}) copy-start(f32[2,64,512]{2,1,0:T(8,128)} %param.15) | copy-start | bytes 786436

commit v5 on v4

--- a/solution.py
+++ b/solution.py
@@ -163,7 +163,8 @@
 
 
 def fused_kernel(
-    counts, blocks, fac_hbm, bf_hbm, bb_hbm, out_f, out_b, out_d,
+    counts_hbm, blocks_hbm, fac_hbm, bf_hbm, bb_hbm, out_f, out_b, out_d,
+    counts, blocks,
     fac, rhs, inv_h, inv_l, y0_h, y0_l, y1_h, y1_l, first, band, diag,
     core_in, held, z_far, z_out, z_near, z_sum, y_in, x_all, full,
     b_far, b_out, b_near, b_send, b_in, b_keep, d_in, d_far, d_out, d_near,
@@ -179,7 +180,7 @@
     net = Net(send_sems, recv_sems)
 
     fac_loads = [pltpu.make_async_copy(fac_hbm.at[t], fac.at[t], load_sems.at[t]) for t in range(cap)]
-    rest = []
+    rest = [(counts_hbm, counts), (blocks_hbm, blocks)]
     for t in range(cap):
         rest.append((bf_hbm.at[t], rhs.at[t, :, pl.ds(0, w)]))
         rest.append((bb_hbm.at[t], rhs.at[t, :, pl.ds(w, w)]))
@@ -397,16 +398,17 @@
     sub = c_band.shape[0]
     zrow = half // 4
     yrow = zrow // 4
-    smem, vmem = pl.BlockSpec(memory_space=pltpu.SMEM), pl.BlockSpec(memory_space=pltpu.VMEM)
+    vmem = pl.BlockSpec(memory_space=pltpu.VMEM)
     hbm = pl.BlockSpec(memory_space=HBM)
     v = lambda *shape: pltpu.VMEM(shape, F32)
     vb = lambda *shape: pltpu.VMEM(shape, BF16)
     return pl.pallas_call(
         fused_kernel,
         out_shape=tuple(jax.ShapeDtypeStruct(a.shape, F32) for a in (c_first, c_band, c_diag)),
-        in_specs=[smem] * 2 + [hbm] * 3,
+        in_specs=[hbm] * 5,
         out_specs=(vmem, vmem, vmem),
         scratch_shapes=[
+            pltpu.SMEM((1,), jnp.int32), pltpu.SMEM((cap,), jnp.int32),
             v(cap, n, n), v(cap, n, 2 * w), vb(cap, n, n), vb(cap, n, n),
             vb(cap, n, w), vb(cap, n, w), vb(cap, n, w), vb(cap, n, w),
             v(w, w), v(4, half, w), v(4, half, w),
@@ -414,20 +416,52 @@
             v(3, yrow, w), v(4, yrow, w), v(w, w),
             v(2, 2, sub, half), v(2, 2, sub, half), v(2, 2, 2, sub, half), v(sub, w), v(sub, w), v(sub, w),
             v(4, k, drow, w), v(2, k, drow, half), v(2, k, drow, half), v(2, 2, k, drow, half),
-            pltpu.SemaphoreType.DMA((3 * cap,)),
+            pltpu.SemaphoreType.DMA((3 * cap + 2,)),
             pltpu.SemaphoreType.DMA((64,)), pltpu.SemaphoreType.DMA((64,)),
         ],
-        compiler_params=pltpu.CompilerParams(vmem_limit_bytes=46 << 20, collective_id=0, has_side_effects=True),
+        compiler_params=pltpu.CompilerParams(vmem_limit_bytes=50 << 20, collective_id=0, has_side_effects=True),
         name="schur",
     )(counts, blocks, factors, b_first, b_branch)
 
 
+def finish_kernel(first, band, diag, cf, cb, cd, out_f, out_b, out_d, tf, tb, td, sems):
+    copies = []
+    half = first.shape[0] // 2
+    for i in range(2):
+        rows = pl.ds(i * half, half)
+        tf[rows] = cf[rows] - first[rows]
+        copies.append(pltpu.make_async_copy(tf.at[rows], out_f.at[rows], sems.at[i]))
+        copies[-1].start()
+    tb[...] = cb[...] - band[...]
+    copies.append(pltpu.make_async_copy(tb, out_b, sems.at[2]))
+    copies[-1].start()
+    td[...] = cd[...] - diag[...]
+    copies.append(pltpu.make_async_copy(td, out_d, sems.at[3]))
+    copies[-1].start()
+    for copy in copies:
+        copy.wait()
+
+
+def finish(first, band, diag, c_first, c_band, c_diag):
+    vmem = pl.BlockSpec(memory_space=pltpu.VMEM)
+    cs = (c_first, c_band, c_diag)
+    return pl.pallas_call(
+        finish_kernel,
+        out_shape=tuple(jax.ShapeDtypeStruct(c.shape, F32) for c in cs),
+        in_specs=[vmem] * 6,
+        out_specs=(pl.BlockSpec(memory_space=HBM),) * 3,
+        scratch_shapes=[pltpu.VMEM(c.shape, F32) for c in cs] + [pltpu.SemaphoreType.DMA((4,))],
+        compiler_params=pltpu.CompilerParams(vmem_limit_bytes=8 << 20),
+        name="finish",
+    )(first, band, diag, *cs)
+
+
 HBM = pltpu.HBM
 
 
 def shards(counts, blocks, factors, b_first, b_branch, c_first, c_band, c_diag):
     first, band, diag = fused(counts, blocks, factors, b_first, b_branch, c_first, c_band, c_diag)
-    return c_first - first, c_band - band, c_diag - diag
+    return finish(first, band, diag, c_first, c_band, c_diag)
 
 
 def solution(mesh):

time: 65.2 us -> 62.9 us (0.965)
  other arithmetic: 2.65 us -> 0 us
  Pallas kernels: 58.2 us -> 60.8 us
  local copies, waits for them, and re-layouts: 2.85 us -> 0.66 us
    sub x3 -> x0, other arithmetic: 2.65 us -> none  [shards(): return (c_first - first, c_band - band, c_diag - diag)]
    unnamed x10 -> x8, local copies, waits for them, and re-layouts: 2.85 us -> 0.66 us
    pallas_call x1, Pallas kernels: 58.2 us -> 59.6 us  [fused(): pl.pallas_call(fused_kernel, out_shape=tuple((jax.ShapeDtypeStruct(a.shap...]
    pallas_call x0 -> x1, Pallas kernels: none -> 1.23 us  [finish(): pl.pallas_call(finish_kernel, out_shape=tuple((jax.ShapeDtypeStruct(c.sha...]
where the time goes in v5:
time: 62.9 us; the launch traced here: 62.8 us
  Pallas kernels  60.8 us (97%)
  between operations  1.32 us (2%)
  local copies, waits for them, and re-layouts  0.66 us (1%)
    pallas_call x1, Pallas kernels, fused(): pl.pallas_call(fused_kernel, out_shape=tuple((jax.ShapeDtypeStruct(a.shap...  59.6 us

profile of v5, /device:TPU:1, one launch (start us, length us, event | category | flops | bytes accessed | tf_op | source)
XLA Modules:
  0.0 62.8 jit_solution(10309002251070206286)
XLA Ops:
  1.3 0.0 copy-start.3
  1.3 0.6 %copy-done.3 = s32[4]{0:T(128)S(1)} copy-done((s32[4]{0:T(128)S(1)}, s32[4]{0:T(128)}, u32[]{:S(2)}) %copy-start.3) | copy-done | bytes 40
  1.9 0.0 copy-start
  1.9 0.0 copy-start.1
  1.9 0.0 copy-start.2
  1.9 59.6 %schur.1 = (f32[512,512]{1,0:T(8,128)S(1)}, f32[128,512]{1,0:T(8,128)S(1)}, f32[2,64,512]{2,1,0:T(8,128)S(1)}) custom-call(s32[1]{0:T(128)S(6)} %copy.11.counts_hbm, s32[4]{0:T(128)S(1)} %copy-done.3, f32[4,512,512]{2,1,0:T(8,128)} %fac_hbm.1, f32[4,512,512]{2,1,0:T(8,128)} %bf_hbm.1, f32[4,512,512]{2,1,0:T(8,128)} %bb_hbm.1), custom_call_target="tpu_custom_call" | custom-call | tf_op jit(solution)/shard_map/schur/pallas_call | solution.py:405
  61.6 0.0 copy-done
  61.6 0.0 copy-done.1
  61.6 0.0 copy-done.2
  61.6 1.2 %finish.1 = (f32[512,512]{1,0:T(8,128)}, f32[128,512]{1,0:T(8,128)}, f32[2,64,512]{2,1,0:T(8,128)}) custom-call(f32[512,512]{1,0:T(8,128)S(1)} %get-tuple-element.6.first, f32[128,512]{1,0:T(8,128)S(1)} %get-tuple-element.7.band, f32[2,64,512]{2,1,0:T(8,128)S(1)} %get-tuple-element.8.diag, f32[512,512]{1,0:T(8,128)S(1)} %copy-done, ...), custom_call_target="tpu_custom_call" | custom-call | tf_op jit(solution)/shard_map/finish/pallas_call | solution.py:448
Async XLA Ops:
  1.3 0.7 %copy-start.3 = (s32[4]{0:T(128)S(1)}, s32[4]{0:T(128)}, u32[]{:S(2)}) copy-start(s32[4]{0:T(128)} %blocks_hbm.1) | copy-start | bytes 52
  1.9 59.6 %copy-start = (f32[512,512]{1,0:T(8,128)S(1)}, f32[512,512]{1,0:T(8,128)}, u32[]{:S(2)}) copy-start(f32[512,512]{1,0:T(8,128)} %cf.1) | copy-start | bytes 3145732
  1.9 59.6 %copy-start.1 = (f32[128,512]{1,0:T(8,128)S(1)}, f32[128,512]{1,0:T(8,128)}, u32[]{:S(2)}) copy-start(f32[128,512]{1,0:T(8,128)} %cb.1) | copy-start | bytes 786436
  1.9 59.6 %copy-start.2 = (f32[2,64,512]{2,1,0:T(8,128)S(1)}, f32[2,64,512]{2,1,0:T(8,128)}, u32[]{:S(2)}) copy-start(f32[2,64,512]{2,1,0:T(8,128)} %cd.1) | copy-start | bytes 786436

commit v6 on v5

--- a/solution.py
+++ b/solution.py
@@ -208,6 +208,13 @@
     for copy in rest_loads:
         copy.wait()
 
+    zrow = half // 4
+    z_ring = Ring(
+        net,
+        lambda role, h: held.at[pl.ds(pl.multiple_of(((z + OFFSETS[role]) % 4) * zrow, zrow), zrow), halves[h]],
+        z_up, z_down, z_far, z_out, z_near,
+    )
+
     first[...] = jnp.zeros_like(first)
 
     def chosen(t, shape):
@@ -224,7 +231,7 @@
             down = dot3(low, right, NN)
             y_h[t, half:, cols], y_l[t, half:, cols] = split(jnp.where(live, down, 0.0))
 
-    @pl.loop(0, cap)
+    @pl.loop(0, cap, unroll=True)
     def _(t):
         solve(t, 0, y0_h, y0_l)
         for i in range(0, w, half):
@@ -240,9 +247,16 @@
     core_rows, core_far = pl.ds(rows_core, half), pl.ds(pl.multiple_of((1 - core) * half, half), half)
     core_copy = net.send(first.at[core_far], core_in, other_core)
 
-    @pl.loop(0, cap)
+    @pl.loop(0, cap - 1, unroll=True)
     def _(t):
         solve(t, w, y1_h, y1_l)
+
+    core_copy.wait_recv()
+    held[...] = first[core_rows] + core_in[...]
+    z_ring.far()
+    z_ring.near_up()
+    z_ring.near_down()
+    solve(cap - 1, w, y1_h, y1_l)
 
     quarter = half // 2
 
@@ -254,7 +268,7 @@
         for role in pair:
             band[role] = jnp.zeros((half, w), F32)
 
-        @pl.loop(0, cap)
+        @pl.loop(0, cap, unroll=True)
         def _(t):
             which = chosen(t, (half, w))
             term = dot3((y1_h[t, :, cols], y1_l[t, :, cols]), (y0_h[t], y0_l[t]), TN)
@@ -266,7 +280,7 @@
         for role in pair:
             diag[role] = jnp.zeros((half, w), F32)
 
-        @pl.loop(0, cap)
+        @pl.loop(0, cap, unroll=True)
         def _(t):
             which = chosen(t, (quarter, w))
             left = [jnp.concatenate([y[t, :, c] for c in cols], axis=1) for y in (y1_h, y1_l)]
@@ -298,18 +312,6 @@
 
     diags = Ring(net, lambda role, h: d_in.at[role, :, :, halves[h]], x_up, x_down, d_far, d_out, d_near)
 
-    zrow = half // 4
-    z_ring = Ring(
-        net,
-        lambda role, h: held.at[pl.ds(pl.multiple_of(((z + OFFSETS[role]) % 4) * zrow, zrow), zrow), halves[h]],
-        z_up, z_down, z_far, z_out, z_near,
-    )
-
-    core_copy.wait_recv()
-    held[...] = first[core_rows] + core_in[...]
-    z_ring.far()
-    z_ring.near_up()
-    z_ring.near_down()
     diag_terms((FAR, OWN))
     d0 = diag_send(FAR)
     z_ring.mid_up()
@@ -317,47 +319,41 @@
     band_terms((FAR, OWN))
     bands[0].far()
     bands[1].far()
-    diag_terms((NEXT, PREV))
     z_sum[:, :half], z_sum[:, half:] = z_ring.end()
     yrow = zrow // 4
     y_copies = []
     for d in (1, 2, 3):
         piece = z_sum.at[pl.ds(pl.multiple_of(((y + d) % 4) * yrow, yrow), yrow)]
         y_copies.append(net.send(piece, y_in.at[d - 1], y_peers[d - 1]))
+    diag_terms((NEXT, PREV))
     d1 = diag_send(NEXT)
     band_terms((NEXT, PREV))
-    bands[0].near_up()
-    bands[0].near_down()
     for copy in y_copies:
         copy.wait_recv()
     own = z_sum[pl.ds(pl.multiple_of(y * yrow, yrow), yrow)]
     x_all[x] = own + y_in[0] + y_in[1] + y_in[2]
     x_copies = [net.send(x_all.at[x], x_all.at[x], peer) for peer in x_peers]
-    d2 = diag_send(PREV)
+    bands[0].near_up()
+    bands[0].near_down()
     bands[0].mid_up()
     bands[0].mid_down()
     diag_take(d0, FAR)
     diags.far()
-    bands[1].near_up()
-    bands[1].near_down()
     for copy in x_copies:
         copy.wait_recv()
     z_rows = rows_core + z * zrow
     y_rows = pl.ds(pl.multiple_of(z_rows + y * yrow, yrow), yrow)
     full[y_rows] = (x_all[0] + x_all[1]) + (x_all[2] + x_all[3])
     y_back = [net.send(full.at[y_rows], full.at[y_rows], peer) for peer in y_peers]
+    d2 = diag_send(PREV)
     d3 = diag_send(OWN)
+    bands[1].near_up()
+    bands[1].near_down()
     bands[1].mid_up()
     bands[1].mid_down()
     diag_take(d1, NEXT)
     diags.near_up()
     diags.mid_up()
-    b_send[:, :half], b_send[:, half:] = bands[0].end()
-    cross = net.send(b_send, b_in, y_near)
-    diag_take(d2, PREV)
-    diags.near_down()
-    diags.mid_down()
-
     for copy in y_back:
         copy.wait_recv()
 
@@ -367,7 +363,8 @@
     mine = full.at[z_block(0)]
     up_copy, down_copy = net.send(mine, mine, z_up), net.send(mine, mine, z_down)
     core_backs = [net.send(mine, mine, other_core)]
-    b_keep[:, :half], b_keep[:, half:] = bands[1].end()
+    b_send[:, :half], b_send[:, half:] = bands[0].end()
+    cross = net.send(b_send, b_in, y_near)
     up_copy.wait_recv()
     below = full.at[z_block(3)]
     pass_up = net.send(full.at[z_block(3), halves[0]], full.at[z_block(3), halves[0]], z_up)
@@ -376,18 +373,22 @@
     above = full.at[z_block(1)]
     pass_down = net.send(full.at[z_block(1), halves[1]], full.at[z_block(1), halves[1]], z_down)
     core_backs.append(net.send(above, above, other_core))
-    diag_take(d3, OWN)
+    diag_take(d2, PREV)
+    diags.near_down()
+    diags.mid_down()
+    b_keep[:, :half], b_keep[:, half:] = bands[1].end()
     pass_up.wait_recv()
     pass_down.wait_recv()
     far = full.at[z_block(2)]
     core_backs.append(net.send(far, far, other_core))
+    diag_take(d3, OWN)
+    for copy in core_backs:
+        copy.wait_recv()
+    out_f[...] = full[...]
     for h, term in enumerate(diags.end()):
         out_d[:, :, halves[h]] = term
     cross.wait_recv()
     out_b[...] = b_keep[...] + b_in[...]
-    for copy in core_backs:
-        copy.wait_recv()
-    out_f[...] = full[...]
     net.drain()
 
 

time: 62.9 us -> 60.8 us (0.967)
  Pallas kernels: 60.8 us -> 58.5 us
    pallas_call x1, Pallas kernels: 59.6 us -> 57.3 us  [fused(): pl.pallas_call(fused_kernel, out_shape=tuple((jax.ShapeDtypeStruct(a.shap...]
where the time goes in v6:
time: 60.8 us; the launch traced here: 60.6 us
  Pallas kernels  58.5 us (96%)
  between operations  1.48 us (2%)
  local copies, waits for them, and re-layouts  0.66 us (1%)
    pallas_call x1, Pallas kernels, fused(): pl.pallas_call(fused_kernel, out_shape=tuple((jax.ShapeDtypeStruct(a.shap...  57.3 us
    pallas_call x1, Pallas kernels, finish(): pl.pallas_call(finish_kernel, out_shape=tuple((jax.ShapeDtypeStruct(c.sha...  1.23 us

profile of v6, /device:TPU:1, one launch (start us, length us, event | category | flops | bytes accessed | tf_op | source)
XLA Modules:
  0.0 60.6 jit_solution(15217867162460665415)
XLA Ops:
  1.3 0.0 copy-start.3
  1.3 0.6 %copy-done.3 = s32[4]{0:T(128)S(1)} copy-done((s32[4]{0:T(128)S(1)}, s32[4]{0:T(128)}, u32[]{:S(2)}) %copy-start.3) | copy-done | bytes 40
  1.9 0.0 copy-start
  1.9 0.0 copy-start.1
  1.9 0.0 copy-start.2
  1.9 57.3 %schur.1 = (f32[512,512]{1,0:T(8,128)S(1)}, f32[128,512]{1,0:T(8,128)S(1)}, f32[2,64,512]{2,1,0:T(8,128)S(1)}) custom-call(s32[1]{0:T(128)S(6)} %copy.11.counts_hbm, s32[4]{0:T(128)S(1)} %copy-done.3, f32[4,512,512]{2,1,0:T(8,128)} %fac_hbm.1, f32[4,512,512]{2,1,0:T(8,128)} %bf_hbm.1, f32[4,512,512]{2,1,0:T(8,128)} %bb_hbm.1), custom_call_target="tpu_custom_call" | custom-call | tf_op jit(solution)/shard_map/schur/pallas_call | solution.py:406
  59.2 0.0 copy-done
  59.2 0.0 copy-done.1
  59.2 0.0 copy-done.2
  59.3 1.2 %finish.1 = (f32[512,512]{1,0:T(8,128)}, f32[128,512]{1,0:T(8,128)}, f32[2,64,512]{2,1,0:T(8,128)}) custom-call(f32[512,512]{1,0:T(8,128)S(1)} %get-tuple-element.6.first, f32[128,512]{1,0:T(8,128)S(1)} %get-tuple-element.7.band, f32[2,64,512]{2,1,0:T(8,128)S(1)} %get-tuple-element.8.diag, f32[512,512]{1,0:T(8,128)S(1)} %copy-done, ...), custom_call_target="tpu_custom_call" | custom-call | tf_op jit(solution)/shard_map/finish/pallas_call | solution.py:449
Async XLA Ops:
  1.3 0.7 %copy-start.3 = (s32[4]{0:T(128)S(1)}, s32[4]{0:T(128)}, u32[]{:S(2)}) copy-start(s32[4]{0:T(128)} %blocks_hbm.1) | copy-start | bytes 52
  1.9 57.3 %copy-start = (f32[512,512]{1,0:T(8,128)S(1)}, f32[512,512]{1,0:T(8,128)}, u32[]{:S(2)}) copy-start(f32[512,512]{1,0:T(8,128)} %cf.1) | copy-start | bytes 3145732
  1.9 57.3 %copy-start.1 = (f32[128,512]{1,0:T(8,128)S(1)}, f32[128,512]{1,0:T(8,128)}, u32[]{:S(2)}) copy-start(f32[128,512]{1,0:T(8,128)} %cb.1) | copy-start | bytes 786436
  1.9 57.3 %copy-start.2 = (f32[2,64,512]{2,1,0:T(8,128)S(1)}, f32[2,64,512]{2,1,0:T(8,128)}, u32[]{:S(2)}) copy-start(f32[2,64,512]{2,1,0:T(8,128)} %cd.1) | copy-start | bytes 786436
